TPU v7x, 32 devices: a whole 2x2x4 slice. The times are simulated.
32 devices in a mesh: cuts: 4 (over z), space: 8 (over y, x, core).
Axes of the slice: x: 2, y: 2, z: 4, core: 2. Of those that a mesh axis runs over, the one named last changes fastest.
Arguments:
- states: float32 [4, 256, 2048], P('cuts', 'space'), may hold values from -6 to 6
- stream: float32 [256, 2048], P('space'), may hold values from -4 to 4
Outputs:
- new_states: float32 [4, 256, 2048], P('cuts', 'space')
All inputs are finite; a program needn't handle non-finite values.
Results may differ from a plain program's by a relative error of at most 0.00002.
Values sent between devices are 32-bit elements; how exact they have to be, the bound alone decides.
No kernel may reach another device: no remote copies, remote signals or barrier semaphores. Data moves between devices by JAX's collectives and lax.ppermute only.
A program may use at most 64 MiB of HBM per device.

v0:
```python
import functools

import jax
import jax.numpy as jnp
from jax import lax
from jax.experimental import pallas as pl
from jax.experimental.pallas import tpu as pltpu
from jax.sharding import PartitionSpec as P

FINE_STEPS = 4
VISCOSITY = 0.2
FINE_DT = 0.25
BLOCK = 4
LANES = 128
SUB = 8
STAGES = 4
REACH = FINE_STEPS * STAGES // 2
SPILL = REACH // BLOCK
VMEM = pl.BlockSpec(memory_space=pltpu.VMEM)
COMPACT = pltpu.CompilerParams(vmem_limit_bytes=12 * 2**20)


def lane_index(shape):
    return lax.broadcasted_iota(jnp.int32, shape, len(shape) - 1)


def horner(diffusion):
    c = 4.0 * diffusion
    b = 24.0**-0.25
    powers = (
        1 - c + c**2 / 2 - c**3 / 6 + c**4 / 24,
        1 - c + c**2 / 2 - c**3 / 6,
        (1 - c + c**2 / 2) / 2,
        (1 - c) / 6,
    )
    return b, [powers[k] / b**k for k in (3, 2, 1, 0)]


def neighbours(source, rows, group):
    tiles = source.shape[0]
    lo, hi = rows
    lane = lane_index((hi - lo, LANES))
    first, last = lane == 0, lane == LANES - 1
    groups = tiles // group

    def eastern(k):
        return pltpu.roll(source[k % groups * group, lo:hi], LANES - 1, 1)

    east_here, west_before = eastern(0), pltpu.roll(source[tiles - 1, lo:hi], 1, 1)
    for k in range(groups):
        east_after = eastern(k + 1)
        here = [source[k * group + i, lo:hi] for i in range(group)]
        west_here = pltpu.roll(here[-1], 1, 1)
        for i in range(group):
            east = here[i + 1] if i + 1 < group else jnp.where(last, east_after, east_here)
            west = here[i - 1] if i else jnp.where(first, west_before, west_here)
            yield k * group + i, east, west
        east_here, west_before = east_after, west_here


def set_coefs(psi, coefs, rows, scale, diffusion, group):
    lo, hi = rows
    b, _ = horner(diffusion)
    scale, diffusion = scale * b, diffusion * b
    for t, east, west in neighbours(psi, rows, group):
        u = scale * (psi[t, lo + 1 : hi + 1] - psi[t, lo - 1 : hi - 1])
        v = scale * (west - east)
        coefs[0, t, lo:hi] = diffusion - u
        coefs[1, t, lo:hi] = diffusion + u
        coefs[2, t, lo:hi] = diffusion - v
        coefs[3, t, lo:hi] = diffusion + v


def stage(source, a, out, coefs, rows, factor, group):
    lo, hi = rows
    for t, east, west in neighbours(source, rows, group):
        along = coefs[0, t, lo:hi] * east + coefs[1, t, lo:hi] * west
        across = coefs[2, t, lo:hi] * source[t, lo + 1 : hi + 1] + coefs[3, t, lo:hi] * source[t, lo - 1 : hi - 1]
        out[t, lo:hi] = (along + across) + factor * a[t, lo:hi]


def step(a, z, coefs, rows, diffusion, group):
    _, factors = horner(diffusion)
    for k in range(STAGES):
        source = a if k == 0 else z.at[(k - 1) % 2]
        stage(source, a, a if k == STAGES - 1 else z.at[k % 2], coefs, rows[k], factors[k], group)


def transposed(parts):
    lane = lane_index(parts[0].shape)
    for width in (LANES // 4, LANES // 2):
        keep = lane // width % 2 == 0
        apart = 4 * width // LANES
        out = list(parts)
        for i in range(4):
            if i & apart == 0:
                j = i + apart
                out[i] = jnp.where(keep, parts[i], pltpu.roll(parts[j], width, 1))
                out[j] = jnp.where(keep, pltpu.roll(parts[i], LANES - width, 1), parts[j])
        parts = out
    return parts


def interleaved(parts):
    lane = lane_index(parts[0].shape)
    at = lane % (LANES // BLOCK) * BLOCK + lane // (LANES // BLOCK)
    return transposed([jnp.take_along_axis(x, at, axis=1) for x in parts])


def in_order(parts):
    lane = lane_index(parts[0].shape)
    at = lane % BLOCK * (LANES // BLOCK) + lane // BLOCK
    return [jnp.take_along_axis(x, at, axis=1) for x in transposed(parts)]


def spread_tiles(source, rows, put):
    lo, hi = rows
    for k in range(0, source.shape[1] // LANES, BLOCK):
        parts = [source[lo:hi, (k + i) * LANES : (k + i + 1) * LANES] for i in range(BLOCK)]
        for i, x in enumerate(interleaved(parts)):
            put(k + i, x)


def pooled(take, tiles, put):
    for k in range(tiles // BLOCK):
        sums = [(take(t, 0) + take(t, 1)) + (take(t, 2) + take(t, 3)) for t in range(k * BLOCK, (k + 1) * BLOCK)]
        put(k, ((sums[0] + sums[1]) + (sums[2] + sums[3])) * (1.0 / (BLOCK * BLOCK)))


def pre_kernel(states, stream, out, *tall):
    rows, cols = states.shape
    count = rows // BLOCK
    for k, source in enumerate((states, stream)):

        def keep(t, value, k=k):
            tall[k][t] = value

        def take(t, i, k=k):
            return tall[k][t, pl.ds(i, count, stride=BLOCK)]

        def put(t, value, k=k):
            out[t, k * count : (k + 1) * count] = value

        spread_tiles(source, (0, rows), keep)
        pooled(take, cols // LANES, put)


def pre_call(states, stream):
    rows, cols = states.shape
    tiles = cols // LANES
    tall = jax.ShapeDtypeStruct((tiles, rows, LANES), jnp.float32)
    return pl.pallas_call(
        pre_kernel,
        out_shape=(jax.ShapeDtypeStruct((tiles // BLOCK, 2 * rows // BLOCK, LANES), jnp.float32), tall, tall),
        in_specs=[VMEM] * 2,
        out_specs=(VMEM,) * 3,
        compiler_params=COMPACT,
        name="restrict",
    )(states, stream)


def fine_kernel(states, stream, low, high, fine, edge_low, edge_high, e_out, a, psi, z, coefs):
    tiles, rows, _ = states.shape
    own = SUB + REACH
    top = own + rows
    size = a.shape[1]
    for k, (buffer, source) in enumerate(((a, states), (psi, stream))):

        def below(t, value, buffer=buffer):
            buffer[t, SUB:own] = value

        def above(t, value, buffer=buffer):
            buffer[t, top : top + REACH] = value

        spread_tiles(low, (k * REACH, (k + 1) * REACH), below)
        spread_tiles(high, (k * REACH, (k + 1) * REACH), above)
        for t in range(tiles):
            buffer[t, own:top] = source[t]
    for t in range(tiles):
        for buffer in (a, psi, z.at[0], z.at[1]):
            buffer[t, 0:SUB] = jnp.zeros((SUB, LANES), jnp.float32)
            buffer[t, top + REACH : size] = jnp.zeros((size - top - REACH, LANES), jnp.float32)
    diffusion = VISCOSITY * FINE_DT
    group = BLOCK
    set_coefs(psi, coefs, (SUB, top + REACH), FINE_DT * 0.25, diffusion, group)

    def rows_at(n):
        reach = REACH - n if n <= REACH else n - REACH
        spare = -(rows + 2 * reach) % SUB
        reach += min(spare // 2, REACH - reach)
        return (own - reach, top + reach)

    half = FINE_STEPS // 2
    for n in range(half):
        step(a, z, coefs, [rows_at(n * STAGES + k) for k in range(1, STAGES + 1)], diffusion, group)
    nothing = jnp.zeros((REACH, LANES), jnp.float32)
    for t in range(tiles):
        for buffer in (a, z.at[0], z.at[1]):
            buffer[t, SUB:own] = nothing
            buffer[t, top : top + REACH] = nothing
    for n in range(half, FINE_STEPS):
        step(a, z, coefs, [rows_at(n * STAGES + k) for k in range(1, STAGES + 1)], diffusion, group)
    for t in range(tiles):
        fine[t] = a[t, own:top]
        edge_low[t] = a[t, SUB:own]
        edge_high[t] = a[t, top : top + REACH]
    spread = e_out.shape[1]

    def take(t, i):
        return a[t, pl.ds(SUB + i, spread, stride=BLOCK)]

    def put(k, value):
        e_out[k] = value

    pooled(take, tiles, put)


def fine_call(states, stream, low, high):
    tiles, rows, _ = states.shape
    spread = -(-(rows // BLOCK + 2 * SPILL) // SUB) * SUB
    size = SUB + max(BLOCK * spread, rows + 2 * REACH + SUB)
    f32 = jnp.float32
    return pl.pallas_call(
        fine_kernel,
        out_shape=(
            jax.ShapeDtypeStruct((tiles, rows, LANES), f32),
            jax.ShapeDtypeStruct((tiles, REACH, LANES), f32),
            jax.ShapeDtypeStruct((tiles, REACH, LANES), f32),
            jax.ShapeDtypeStruct((tiles // BLOCK, spread, LANES), f32),
        ),
        in_specs=[VMEM] * 4,
        out_specs=(VMEM,) * 4,
        scratch_shapes=[
            pltpu.VMEM((tiles, size, LANES), f32),
            pltpu.VMEM((tiles, size, LANES), f32),
            pltpu.VMEM((2, tiles, size, LANES), f32),
            pltpu.VMEM((4, tiles, size, LANES), f32),
        ],
        compiler_params=COMPACT,
        name="fine",
    )(states, stream, low, high)


def pair_kernel(mine, theirs, out):
    tiles, both, _ = mine.shape
    rows = both // 2
    odd = lax.rem(lax.axis_index("space"), 2) == 1
    for t in range(tiles):
        lower = jnp.where(odd, theirs[t], mine[t])
        upper = jnp.where(odd, mine[t], theirs[t])
        for k in range(2):
            out[t, 2 * k * rows : (2 * k + 1) * rows] = lower[k * rows : (k + 1) * rows]
            out[t, (2 * k + 1) * rows : (2 * k + 2) * rows] = upper[k * rows : (k + 1) * rows]


def pair_call(mine, theirs):
    tiles, both, _ = mine.shape
    return pl.pallas_call(
        pair_kernel,
        out_shape=jax.ShapeDtypeStruct((tiles, 2 * both, LANES), jnp.float32),
        in_specs=[VMEM] * 2,
        out_specs=VMEM,
        compiler_params=COMPACT,
        name="pair",
    )(mine, theirs)


def spread_kernel(rows, mine, theirs, whole, message):
    tiles, spread, _ = mine.shape
    odd = lax.rem(lax.axis_index("space"), 2) == 1
    for t in range(tiles):
        lower = jnp.where(odd, theirs[t], mine[t])
        upper = jnp.where(odd, mine[t], theirs[t])
        whole[t, 0:spread] = lower
        whole[t, spread:] = jnp.zeros((whole.shape[1] - spread, LANES), jnp.float32)
        whole[t, rows : rows + spread] = whole[t, rows : rows + spread] + upper
        message[t] = jnp.where(odd, whole[t, 2 * SPILL : 2 * SPILL + 2 * rows], whole[t, 0 : 2 * rows])


def spread_call(mine, theirs, rows):
    tiles, spread, _ = mine.shape
    f32 = jnp.float32
    return pl.pallas_call(
        functools.partial(spread_kernel, rows),
        out_shape=(
            jax.ShapeDtypeStruct((tiles, rows + spread, LANES), f32),
            jax.ShapeDtypeStruct((tiles, 2 * rows, LANES), f32),
        ),
        in_specs=[VMEM] * 2,
        out_specs=(VMEM,) * 2,
        compiler_params=COMPACT,
        name="spread",
    )(mine, theirs)


def partner(n, k, size):
    return n ^ k if size & (size - 1) == 0 else (n + k) % size


def chain(pads, outs, rows, scratch):
    gap, old, psi, z, coefs, powers = scratch
    tiles, size, _ = gap.shape
    spacing, length = float(BLOCK), FINE_DT * FINE_STEPS
    diffusion = VISCOSITY * length / (spacing * spacing)
    whole = (SUB, size - SUB)
    base = SUB + pads
    slices = len(outs)
    own = base + pl.multiple_of(rows * lax.rem(lax.axis_index("space"), 2), SUB)
    group = 1
    set_coefs(psi, coefs, whole, length / (2.0 * spacing) / (2.0 * spacing), diffusion, group)
    step(old, z, coefs, [whole] * STAGES, diffusion, group)
    n = lax.axis_index("cuts")
    for t in range(tiles):
        start = jnp.where(n == 0, old[t, whole[0] : whole[1]], 0.0)
        gap[t, whole[0] : whole[1]] = (gap[t, whole[0] : whole[1]] - old[t, whole[0] : whole[1]]) + start
        mine = old[t, pl.ds(own, rows)]
        outs[-1][t] = jnp.where(n == 0, mine, 0.0) - mine
    reach = STAGES * (slices - 1)

    def around(extent):
        extent = min(-(-extent // SUB) * SUB, pads)
        return (base - extent, base + 2 * rows + extent)

    for j in range(1, slices):
        reach -= STAGES
        step(gap, z, coefs, [around(reach + STAGES - k) for k in range(1, STAGES + 1)], diffusion, group)
        for t in range(tiles):
            powers[j, t] = gap[t, pl.ds(own, rows)]
    for k in range(1, slices):
        ahead = jnp.clip(partner(n, k, slices) - n, 1, slices - 1)
        for t in range(tiles):
            outs[k - 1][t] = powers[ahead, t]


def pair_chain_kernel(slices, rows, whole, message, passed, coarse, coarse_near, coarse_far, *refs):
    outs, scratch = refs[:slices], refs[slices:]
    gap, old, psi, z = scratch[:4]
    tiles = gap.shape[0]
    size = gap.shape[1]
    odd = lax.rem(lax.axis_index("space"), 2) == 1
    pads = 2 * rows
    base = SUB + pads
    edge = jnp.zeros((SUB, LANES), jnp.float32)
    for t in range(tiles):
        before, after = jnp.where(odd, passed[t], message[t]), jnp.where(odd, message[t], passed[t])
        gap[t] = jnp.zeros((size, LANES), jnp.float32)
        at = base - SPILL
        gap[t, at : at + whole.shape[1]] = whole[t]
        at = base + SPILL - 2 * rows
        gap[t, at : at + 2 * rows] = gap[t, at : at + 2 * rows] + before
        at = base - SPILL + 2 * rows
        gap[t, at : at + 2 * rows] = gap[t, at : at + 2 * rows] + after
        before = jnp.where(odd, coarse_far[t], coarse_near[t])
        after = jnp.where(odd, coarse_near[t], coarse_far[t])
        for k, out in ((0, old), (1, psi)):
            part = slice(2 * k * rows, 2 * (k + 1) * rows)
            out[t, 0:SUB] = edge
            out[t, SUB:base] = before[part]
            out[t, base : base + 2 * rows] = coarse[t, part]
            out[t, base + 2 * rows : base + 4 * rows] = after[part]
            out[t, size - SUB : size] = edge
        for k in range(2):
            z[k, t, 0:SUB] = edge
            z[k, t, size - SUB : size] = edge
    chain(pads, outs, rows, scratch)


def chain_scratch(tiles, size, slices, rows):
    f32 = jnp.float32
    return [
        pltpu.VMEM((tiles, size, LANES), f32),
        pltpu.VMEM((tiles, size, LANES), f32),
        pltpu.VMEM((tiles, size, LANES), f32),
        pltpu.VMEM((2, tiles, size, LANES), f32),
        pltpu.VMEM((4, tiles, size, LANES), f32),
        pltpu.VMEM((slices, tiles, rows, LANES), f32),
    ]


def pair_chain_call(slices, whole, message, passed, coarse, coarse_near, coarse_far):
    tiles = whole.shape[0]
    rows = message.shape[1] // 2
    return pl.pallas_call(
        functools.partial(pair_chain_kernel, slices, rows),
        out_shape=(jax.ShapeDtypeStruct((tiles, rows, LANES), jnp.float32),) * slices,
        in_specs=[VMEM] * 6,
        out_specs=(VMEM,) * slices,
        scratch_shapes=chain_scratch(tiles, 6 * rows + 2 * SUB, slices, rows),
        compiler_params=COMPACT,
        name="coarse",
    )(whole, message, passed, coarse, coarse_near, coarse_far)


def wide_chain_kernel(slices, rows, gap_in, old_in, psi_in, *refs):
    outs, scratch = refs[:slices], refs[slices:]
    gap, old, psi, z = scratch[:4]
    tiles, size, _ = gap.shape
    edge = jnp.zeros((SUB, LANES), jnp.float32)
    for t in range(tiles):
        for source, out in ((gap_in, gap), (old_in, old), (psi_in, psi)):
            out[t, 0:SUB] = edge
            out[t, SUB : size - SUB] = source[t]
            out[t, size - SUB : size] = edge
        for k in range(2):
            z[k, t, 0:SUB] = edge
            z[k, t, size - SUB : size] = edge
    chain((size - 2 * SUB - 2 * rows) // 2, outs, rows, scratch)


def wide_chain(slices, spread, coarse):
    tiles, both, _ = coarse.shape
    rows = both // 2
    bands = lax.axis_size("space")
    total = bands * rows
    length = spread.shape[1]
    every = lax.all_gather(spread, "space")
    gap = jnp.zeros((tiles, total, LANES), jnp.float32)
    for b in range(bands):
        at = (b * rows - SPILL + jnp.arange(length)) % total
        gap = gap.at[:, at].add(every[b])
    every = lax.all_gather(coarse, "space")
    old, psi = (jnp.moveaxis(every[:, :, k * rows : (k + 1) * rows], 0, 1).reshape(tiles, total, LANES) for k in range(2))
    pads = STAGES * slices
    first = lax.axis_index("space") // 2 * 2 * rows
    at = (first - pads + jnp.arange(2 * rows + 2 * pads)) % total
    size = 2 * rows + 2 * pads + 2 * SUB
    return pl.pallas_call(
        functools.partial(wide_chain_kernel, slices, rows),
        out_shape=(jax.ShapeDtypeStruct((tiles, rows, LANES), jnp.float32),) * slices,
        in_specs=[VMEM] * 3,
        out_specs=(VMEM,) * slices,
        scratch_shapes=chain_scratch(tiles, size, slices, rows),
        compiler_params=COMPACT,
        name="coarse",
    )(*(jnp.take(x, at, axis=1) for x in (gap, old, psi)))


def settle_kernel(fine, from_low, from_high, out, tall):
    tiles, rows, _ = fine.shape
    for t in range(tiles):
        tall[t, 0:REACH] = fine[t, 0:REACH] + from_low[t]
        tall[t, REACH : rows - REACH] = fine[t, REACH : rows - REACH]
        tall[t, rows - REACH : rows] = fine[t, rows - REACH : rows] + from_high[t]
    for k in range(0, tiles, BLOCK):
        for i, x in enumerate(in_order([tall[k + i] for i in range(BLOCK)])):
            out[:, (k + i) * LANES : (k + i + 1) * LANES] = x


def settle_call(fine, from_low, from_high):
    tiles, rows, _ = fine.shape
    return pl.pallas_call(
        settle_kernel,
        out_shape=jax.ShapeDtypeStruct((rows, tiles * LANES), jnp.float32),
        in_specs=[VMEM] * 3,
        out_specs=VMEM,
        scratch_shapes=[pltpu.VMEM((tiles, rows, LANES), jnp.float32)],
        compiler_params=COMPACT,
        name="settle",
    )(fine, from_low, from_high)


def out_kernel(slices, fine, own, *refs):
    received, (out, tall) = refs[: slices - 1], refs[slices - 1 :]
    rows, cols = fine.shape
    count = rows // BLOCK
    n = lax.axis_index("cuts")
    lane = lane_index((count, LANES))
    per = LANES // BLOCK
    sources = [(n ^ k) if slices & (slices - 1) == 0 else lax.rem(n + slices - k, slices) for k in range(1, slices)]
    for k in range(cols // LANES // BLOCK):
        total = own[k]
        for source, x in zip(sources, received, strict=True):
            total = total + jnp.where(source < n, x[k], 0.0)
        for q in range(BLOCK):
            t = k * BLOCK + q
            up = jnp.take_along_axis(total, q * per + lane // BLOCK, axis=1)
            for i in range(BLOCK):
                tall[t, pl.ds(i, count, stride=BLOCK)] = up
            at = slice(t * LANES, (t + 1) * LANES)
            out[0, :, at] = fine[:, at] + tall[t]


def out_call(slices, fine, own, received):
    rows, cols = fine.shape
    return pl.pallas_call(
        functools.partial(out_kernel, slices),
        out_shape=jax.ShapeDtypeStruct((1, rows, cols), jnp.float32),
        in_specs=[VMEM] * (1 + slices),
        out_specs=VMEM,
        scratch_shapes=[pltpu.VMEM((cols // LANES, rows, LANES), jnp.float32)],
        compiler_params=COMPACT,
        name="total",
    )(fine, own, *received)


def iteration(states, stream):
    state = states[0]
    slices, bands = lax.axis_size("cuts"), lax.axis_size("space")
    rows = state.shape[0] // BLOCK
    up = [(i, (i + 1) % bands) for i in range(bands)]
    down = [(i, (i - 1) % bands) for i in range(bands)]
    twin = [(i, i ^ 1) for i in range(bands)]
    across = [(i, (i + 1 if i % 2 else i - 1) % bands) for i in range(bands)]

    def exchange(x, pairs):
        return lax.ppermute(x, "space", pairs)

    low = exchange(jnp.concatenate([state[-REACH:], stream[-REACH:]]), up)
    high = exchange(jnp.concatenate([state[:REACH], stream[:REACH]]), down)
    coarse, state, stream = pre_call(state, stream)
    paired = bands % 2 == 0 and STAGES * (slices - 1) <= 2 * rows - SPILL
    if paired:
        coarse = pair_call(coarse, exchange(coarse, twin))
        coarse_near = exchange(coarse, across)
        coarse_far = exchange(coarse_near, twin)
    fine, edge_low, edge_high, spread = fine_call(state, stream, low, high)
    if paired:
        whole, message = spread_call(spread, exchange(spread, twin), rows)
        near = exchange(message, across)
        far = exchange(near, twin)
        from_low, from_high = exchange(edge_high, up), exchange(edge_low, down)
        *sent, own = pair_chain_call(slices, whole, near, far, coarse, coarse_near, coarse_far)
    else:
        from_low, from_high = exchange(edge_high, up), exchange(edge_low, down)
        *sent, own = wide_chain(slices, spread, coarse)
    received = []
    for k, x in enumerate(sent, 1):
        received.append(lax.ppermute(x, "cuts", [(i, partner(i, k, slices)) for i in range(slices)]))
    return out_call(slices, settle_call(fine, from_low, from_high), own, received)


def solution(mesh):
    return jax.shard_map(
        iteration,
        mesh=mesh,
        in_specs=(P("cuts", "space", None), P("space", None)),
        out_specs=P("cuts", "space", None),
        check_vma=False,
    )
```

profile of v0, /device:TPU:0, one launch (start us, length us, event | category | flops | bytes accessed | tf_op | source)
XLA Modules:
  0.0 32.1 jit_solution(16579270014050169013)
XLA Ops:
  0.0 0.0 copy-start.1
  0.0 0.9 %slice_bitcast_fusion = (f32[8,2048]{1,0:T(8,128)S(1)}, f32[8,2048]{1,0:T(8,128)S(1)}) fusion(f32[1,32,2048]{2,1,0:T(8,128)} %param.2), kind=kLoop, calls=%fused_computation.2 | loop fusion | bytes 262144 | tf_op jit(solution)/shard_map/slice | solution.py:509
  0.9 0.1 copy-done.1
  1.0 0.0 copy-start
  1.1 0.5 %collective-permute-start = (f32[16,2048]{1,0:T(8,128)S(1)}, f32[16,2048]{1,0:T(8,128)S(1)}, u32[]{:S(2)}, u32[]{:S(2)}) collective-permute-start(f32[16,2048]{1,0:T(8,128)S(1)} %pad_maximum_fusion), channel_id=1, source_target_pairs={{0,1},{1,2},{2,3},{3,4},{4,5},{5,6},{6,7},{7,0},{8,9},{9,10},{10,1... | collective-permute-start | bytes 393224 | tf_op jit(solution)/shard_map/ppermute | solution.py:506
  1.6 2.9 %collective-permute-start.1 = (f32[16,2048]{1,0:T(8,128)S(1)}, f32[16,2048]{1,0:T(8,128)S(1)}, u32[]{:S(2)}, u32[]{:S(2)}) collective-permute-start(f32[16,2048]{1,0:T(8,128)S(1)} %pad_maximum_fusion.1), channel_id=1, source_target_pairs={{0,7},{1,0},{2,1},{3,2},{4,3},{5,4},{6,5},{7,6},{8,15},{9,8},{10,9... | collective-permute-start | bytes 393224 | tf_op jit(solution)/shard_map/ppermute | solution.py:506
  4.6 0.0 copy-done
  4.6 1.1 %restrict.1 = (f32[4,16,128]{2,1,0:T(8,128)S(1)}, f32[16,32,128]{2,1,0:T(8,128)S(1)}, f32[16,32,128]{2,1,0:T(8,128)S(1)}) custom-call(f32[32,2048]{1,0:T(8,128)S(1)} %bitcast.5, f32[32,2048]{1,0:T(8,128)S(1)} %copy-done.1), custom_call_target="tpu_custom_call" | custom-call | tf_op jit(solution)/shard_map/restrict/pallas_call | solution.py:152
  5.6 0.1 collective-permute-start.7
  5.7 1.2 %collective-permute-done.7.theirs = f32[4,16,128]{2,1,0:T(8,128)S(1)} collective-permute-done((f32[4,16,128]{2,1,0:T(8,128)S(1)}, f32[4,16,128]{2,1,0:T(8,128)S(1)}, u32[]{:S(2)}, u32[]{:S(2)}) %collective-permute-start.7) | collective-permute-done | bytes 32800 | tf_op jit(solution)/shard_map/ppermute | solution.py:506
  6.9 2.1 %collective-permute-start.8 = (f32[4,32,128]{2,1,0:T(8,128)S(1)}, f32[4,32,128]{2,1,0:T(8,128)S(1)}, u32[]{:S(2)}, u32[]{:S(2)}) collective-permute-start(f32[4,32,128]{2,1,0:T(8,128)S(1)} %pair.1.coarse), channel_id=1, source_target_pairs={{0,7},{1,2},{2,1},{3,4},{4,3},{5,6},{6,5},{7,0},{8,15},{9,10},{10,... | collective-permute-start | bytes 196616 | tf_op jit(solution)/shard_map/ppermute | solution.py:506
  9.0 0.0 collective-permute-done.low
  9.0 0.0 collective-permute-done.1.high
  9.0 3.8 %fine.1 = (f32[16,32,128]{2,1,0:T(8,128)S(1)}, f32[16,8,128]{2,1,0:T(8,128)S(1)}, f32[16,8,128]{2,1,0:T(8,128)S(1)}, f32[4,16,128]{2,1,0:T(8,128)S(1)}) custom-call(f32[16,32,128]{2,1,0:T(8,128)S(1)} %get-tuple-element.18.states, f32[16,32,128]{2,1,0:T(8,128)S(1)} %get-tuple-element.19.stream, f32[16,2048]{1,0:T(8,128)S(1)} %collective-permute-done.low, ...), custom_call_target="tpu_custom_call" | custom-call | tf_op jit(solution)/shard_map/fine/pallas_call | solution.py:223
  12.8 0.2 collective-permute-start.4
  13.0 0.0 collective-permute-done.8.coarse_near
  13.0 0.4 %collective-permute-start.9 = (f32[4,32,128]{2,1,0:T(8,128)S(1)}, f32[4,32,128]{2,1,0:T(8,128)S(1)}, u32[]{:S(2)}, u32[]{:S(2)}) collective-permute-start(f32[4,32,128]{2,1,0:T(8,128)S(1)} %collective-permute-done.8.coarse_near), channel_id=1, source_target_pairs={{0,1},{1,0},{2,3},{3,2},{4,5},{5,4},{6,7},{7,6},{8,9},{9,8},{10,11... | collective-permute-start | bytes 196616 | tf_op jit(solution)/shard_map/ppermute | solution.py:506
  13.4 0.7 %collective-permute-done.4.theirs = f32[4,16,128]{2,1,0:T(8,128)S(1)} collective-permute-done((f32[4,16,128]{2,1,0:T(8,128)S(1)}, f32[4,16,128]{2,1,0:T(8,128)S(1)}, u32[]{:S(2)}, u32[]{:S(2)}) %collective-permute-start.4) | collective-permute-done | bytes 32800 | tf_op jit(solution)/shard_map/ppermute | solution.py:506
  14.1 1.3 %collective-permute-start.5 = (f32[4,16,128]{2,1,0:T(8,128)S(1)}, f32[4,16,128]{2,1,0:T(8,128)S(1)}, u32[]{:S(2)}, u32[]{:S(2)}) collective-permute-start(f32[4,16,128]{2,1,0:T(8,128)S(1)} %get-tuple-element.25), channel_id=1, source_target_pairs={{0,7},{1,2},{2,1},{3,4},{4,3},{5,6},{6,5},{7,0},{8,15},{9,10},{10,... | collective-permute-start | bytes 98312 | tf_op jit(solution)/shard_map/ppermute | solution.py:506
  15.4 0.6 %collective-permute-start.2 = (f32[16,8,128]{2,1,0:T(8,128)S(1)}, f32[16,8,128]{2,1,0:T(8,128)S(1)}, u32[]{:S(2)}, u32[]{:S(2)}) collective-permute-start(f32[16,8,128]{2,1,0:T(8,128)S(1)} %get-tuple-element.21), channel_id=1, source_target_pairs={{0,1},{1,2},{2,3},{3,4},{4,5},{5,6},{6,7},{7,0},{8,9},{9,10},{10,1... | collective-permute-start | bytes 196616 | tf_op jit(solution)/shard_map/ppermute | solution.py:506
  16.0 2.1 %collective-permute-start.3 = (f32[16,8,128]{2,1,0:T(8,128)S(1)}, f32[16,8,128]{2,1,0:T(8,128)S(1)}, u32[]{:S(2)}, u32[]{:S(2)}) collective-permute-start(f32[16,8,128]{2,1,0:T(8,128)S(1)} %get-tuple-element.22), channel_id=1, source_target_pairs={{0,7},{1,0},{2,1},{3,2},{4,3},{5,4},{6,5},{7,6},{8,15},{9,8},{10,9... | collective-permute-start | bytes 196616 | tf_op jit(solution)/shard_map/ppermute | solution.py:506
  18.0 0.6 %collective-permute-done.5.message = f32[4,16,128]{2,1,0:T(8,128)S(1)} collective-permute-done((f32[4,16,128]{2,1,0:T(8,128)S(1)}, f32[4,16,128]{2,1,0:T(8,128)S(1)}, u32[]{:S(2)}, u32[]{:S(2)}) %collective-permute-start.5) | collective-permute-done | bytes 32800 | tf_op jit(solution)/shard_map/ppermute | solution.py:506
  18.6 0.0 collective-permute-start.6
  18.6 0.0 collective-permute-done.9.coarse_far
  18.6 1.2 %collective-permute-done.6.passed = f32[4,16,128]{2,1,0:T(8,128)S(1)} collective-permute-done((f32[4,16,128]{2,1,0:T(8,128)S(1)}, f32[4,16,128]{2,1,0:T(8,128)S(1)}, u32[]{:S(2)}, u32[]{:S(2)}) %collective-permute-start.6) | collective-permute-done | bytes 32800 | tf_op jit(solution)/shard_map/ppermute | solution.py:506
  19.8 1.7 %coarse.1 = (f32[4,8,128]{2,1,0:T(8,128)S(1)}, f32[4,8,128]{2,1,0:T(8,128)S(1)}, f32[4,8,128]{2,1,0:T(8,128)S(1)}, f32[4,8,128]{2,1,0:T(8,128)S(1)}) custom-call(f32[4,24,128]{2,1,0:T(8,128)S(1)} %get-tuple-element.24.whole, f32[4,16,128]{2,1,0:T(8,128)S(1)} %collective-permute-done.5.message, f32[4,16,128]{2,1,0:T(8,128)S(1)} %collective-permute-done.6.passed, ...), custom_call_target="tpu_custom_call" | custom-call | tf_op jit(solution)/shard_map/coarse/pallas_call | solution.py:383
  21.5 1.6 %collective-permute-start.10 = (f32[4,8,128]{2,1,0:T(8,128)S(1)}, f32[4,8,128]{2,1,0:T(8,128)S(1)}, u32[]{:S(2)}, u32[]{:S(2)}) collective-permute-start(f32[4,8,128]{2,1,0:T(8,128)S(1)} %get-tuple-element.28), channel_id=1, source_target_pairs={{0,8},{8,0},{16,24},{24,16},{1,9},{9,1},{17,25},{25,17},{2,10},{10... | collective-permute-start | bytes 49160 | tf_op jit(solution)/shard_map/ppermute | solution.py:528
  23.2 2.6 %collective-permute-start.11 = (f32[4,8,128]{2,1,0:T(8,128)S(1)}, f32[4,8,128]{2,1,0:T(8,128)S(1)}, u32[]{:S(2)}, u32[]{:S(2)}) collective-permute-start(f32[4,8,128]{2,1,0:T(8,128)S(1)} %get-tuple-element.29), channel_id=1, source_target_pairs={{0,16},{8,24},{16,0},{24,8},{1,17},{9,25},{17,1},{25,9},{2,18},{10... | collective-permute-start | bytes 49160 | tf_op jit(solution)/shard_map/ppermute | solution.py:528
  25.8 0.2 collective-permute-start.12
  26.0 0.0 collective-permute-done.2.from_low
  26.0 0.0 collective-permute-done.3.from_high
  26.0 0.5 %settle.1.fine = f32[32,2048]{1,0:T(8,128)S(1)} custom-call(f32[16,32,128]{2,1,0:T(8,128)S(1)} %get-tuple-element.20.fine, f32[16,8,128]{2,1,0:T(8,128)S(1)} %collective-permute-done.2.from_low, f32[16,8,128]{2,1,0:T(8,128)S(1)} %collective-permute-done.3.from_high), custom_call_target="tpu_custom_call" | custom-call | tf_op jit(solution)/shard_map/settle/pallas_call | solution.py:451
  26.5 0.0 collective-permute-done.10.refs_0_
  26.5 1.4 %collective-permute-done.11.refs_1_ = f32[4,8,128]{2,1,0:T(8,128)S(1)} collective-permute-done((f32[4,8,128]{2,1,0:T(8,128)S(1)}, f32[4,8,128]{2,1,0:T(8,128)S(1)}, u32[]{:S(2)}, u32[]{:S(2)}) %collective-permute-start.11) | collective-permute-done | bytes 16416 | tf_op jit(solution)/shard_map/ppermute | solution.py:528
  27.9 3.4 %collective-permute-done.12.refs_2_ = f32[4,8,128]{2,1,0:T(8,128)S(1)} collective-permute-done((f32[4,8,128]{2,1,0:T(8,128)S(1)}, f32[4,8,128]{2,1,0:T(8,128)S(1)}, u32[]{:S(2)}, u32[]{:S(2)}) %collective-permute-start.12) | collective-permute-done | bytes 16416 | tf_op jit(solution)/shard_map/ppermute | solution.py:528
  31.3 0.8 %total.1 = f32[1,32,2048]{2,1,0:T(8,128)} custom-call(f32[32,2048]{1,0:T(8,128)S(1)} %settle.1.fine, f32[4,8,128]{2,1,0:T(8,128)S(1)} %get-tuple-element.27.own, f32[4,8,128]{2,1,0:T(8,128)S(1)} %collective-permute-done.10.refs_0_, f32[4,8,128]{2,1,0:T(8,128)S(1)} %collective-permute-done.11.refs_1_, f32[4,8,128]{2,1,0:T(8,128)S(1)} %collective-permute-done.12.refs_2_), custom_call_target="tpu_custom_call" | custom-call | tf_op jit(solution)/shard_map/total/pallas_call | solution.py:485
  (5 shorter events, 0.1 us)
Async XLA Ops:
  0.0 1.0 %copy-start.1 = (f32[32,2048]{1,0:T(8,128)S(1)}, f32[32,2048]{1,0:T(8,128)}, u32[]{:S(2)}) copy-start(f32[32,2048]{1,0:T(8,128)} %stream.1) | copy-start | bytes 786436
  1.0 3.5 %copy-start = (f32[1,32,2048]{2,1,0:T(8,128)S(1)}, f32[1,32,2048]{2,1,0:T(8,128)}, u32[]{:S(2)}) copy-start(f32[1,32,2048]{2,1,0:T(8,128)} %param.2) | copy-start | bytes 786436
  1.1 8.0 %collective-permute-start = (f32[16,2048]{1,0:T(8,128)S(1)}, f32[16,2048]{1,0:T(8,128)S(1)}, u32[]{:S(2)}, u32[]{:S(2)}) collective-permute-start(f32[16,2048]{1,0:T(8,128)S(1)} %pad_maximum_fusion), channel_id=1, source_target_pairs={{0,1},{1,2},{2,3},{3,4},{4,5},{5,6},{6,7},{7,0},{8,9},{9,10},{10,1... | collective-permute-start | bytes 393224 | tf_op jit(solution)/shard_map/ppermute | solution.py:506
  1.6 7.4 %collective-permute-start.1 = (f32[16,2048]{1,0:T(8,128)S(1)}, f32[16,2048]{1,0:T(8,128)S(1)}, u32[]{:S(2)}, u32[]{:S(2)}) collective-permute-start(f32[16,2048]{1,0:T(8,128)S(1)} %pad_maximum_fusion.1), channel_id=1, source_target_pairs={{0,7},{1,0},{2,1},{3,2},{4,3},{5,4},{6,5},{7,6},{8,15},{9,8},{10,9... | collective-permute-start | bytes 393224 | tf_op jit(solution)/shard_map/ppermute | solution.py:506
  5.6 1.3 %collective-permute-start.7 = (f32[4,16,128]{2,1,0:T(8,128)S(1)}, f32[4,16,128]{2,1,0:T(8,128)S(1)}, u32[]{:S(2)}, u32[]{:S(2)}) collective-permute-start(f32[4,16,128]{2,1,0:T(8,128)S(1)} %get-tuple-element.26.mine), channel_id=1, source_target_pairs={{0,1},{1,0},{2,3},{3,2},{4,5},{5,4},{6,7},{7,6},{8,9},{9,8},{10,11... | collective-permute-start | bytes 98312 | tf_op jit(solution)/shard_map/ppermute | solution.py:506
  6.9 6.1 %collective-permute-start.8 = (f32[4,32,128]{2,1,0:T(8,128)S(1)}, f32[4,32,128]{2,1,0:T(8,128)S(1)}, u32[]{:S(2)}, u32[]{:S(2)}) collective-permute-start(f32[4,32,128]{2,1,0:T(8,128)S(1)} %pair.1.coarse), channel_id=1, source_target_pairs={{0,7},{1,2},{2,1},{3,4},{4,3},{5,6},{6,5},{7,0},{8,15},{9,10},{10,... | collective-permute-start | bytes 196616 | tf_op jit(solution)/shard_map/ppermute | solution.py:506
  12.8 1.3 %collective-permute-start.4 = (f32[4,16,128]{2,1,0:T(8,128)S(1)}, f32[4,16,128]{2,1,0:T(8,128)S(1)}, u32[]{:S(2)}, u32[]{:S(2)}) collective-permute-start(f32[4,16,128]{2,1,0:T(8,128)S(1)} %get-tuple-element.23.mine), channel_id=1, source_target_pairs={{0,1},{1,0},{2,3},{3,2},{4,5},{5,4},{6,7},{7,6},{8,9},{9,8},{10,11... | collective-permute-start | bytes 98312 | tf_op jit(solution)/shard_map/ppermute | solution.py:506
  13.0 5.6 %collective-permute-start.9 = (f32[4,32,128]{2,1,0:T(8,128)S(1)}, f32[4,32,128]{2,1,0:T(8,128)S(1)}, u32[]{:S(2)}, u32[]{:S(2)}) collective-permute-start(f32[4,32,128]{2,1,0:T(8,128)S(1)} %collective-permute-done.8.coarse_near), channel_id=1, source_target_pairs={{0,1},{1,0},{2,3},{3,2},{4,5},{5,4},{6,7},{7,6},{8,9},{9,8},{10,11... | collective-permute-start | bytes 196616 | tf_op jit(solution)/shard_map/ppermute | solution.py:506
  14.1 4.5 %collective-permute-start.5 = (f32[4,16,128]{2,1,0:T(8,128)S(1)}, f32[4,16,128]{2,1,0:T(8,128)S(1)}, u32[]{:S(2)}, u32[]{:S(2)}) collective-permute-start(f32[4,16,128]{2,1,0:T(8,128)S(1)} %get-tuple-element.25), channel_id=1, source_target_pairs={{0,7},{1,2},{2,1},{3,4},{4,3},{5,6},{6,5},{7,0},{8,15},{9,10},{10,... | collective-permute-start | bytes 98312 | tf_op jit(solution)/shard_map/ppermute | solution.py:506
  15.4 10.6 %collective-permute-start.2 = (f32[16,8,128]{2,1,0:T(8,128)S(1)}, f32[16,8,128]{2,1,0:T(8,128)S(1)}, u32[]{:S(2)}, u32[]{:S(2)}) collective-permute-start(f32[16,8,128]{2,1,0:T(8,128)S(1)} %get-tuple-element.21), channel_id=1, source_target_pairs={{0,1},{1,2},{2,3},{3,4},{4,5},{5,6},{6,7},{7,0},{8,9},{9,10},{10,1... | collective-permute-start | bytes 196616 | tf_op jit(solution)/shard_map/ppermute | solution.py:506
  16.0 10.0 %collective-permute-start.3 = (f32[16,8,128]{2,1,0:T(8,128)S(1)}, f32[16,8,128]{2,1,0:T(8,128)S(1)}, u32[]{:S(2)}, u32[]{:S(2)}) collective-permute-start(f32[16,8,128]{2,1,0:T(8,128)S(1)} %get-tuple-element.22), channel_id=1, source_target_pairs={{0,7},{1,0},{2,1},{3,2},{4,3},{5,4},{6,5},{7,6},{8,15},{9,8},{10,9... | collective-permute-start | bytes 196616 | tf_op jit(solution)/shard_map/ppermute | solution.py:506
  18.6 1.2 %collective-permute-start.6 = (f32[4,16,128]{2,1,0:T(8,128)S(1)}, f32[4,16,128]{2,1,0:T(8,128)S(1)}, u32[]{:S(2)}, u32[]{:S(2)}) collective-permute-start(f32[4,16,128]{2,1,0:T(8,128)S(1)} %collective-permute-done.5.message), channel_id=1, source_target_pairs={{0,1},{1,0},{2,3},{3,2},{4,5},{5,4},{6,7},{7,6},{8,9},{9,8},{10,11... | collective-permute-start | bytes 98312 | tf_op jit(solution)/shard_map/ppermute | solution.py:506
  21.5 4.9 %collective-permute-start.10 = (f32[4,8,128]{2,1,0:T(8,128)S(1)}, f32[4,8,128]{2,1,0:T(8,128)S(1)}, u32[]{:S(2)}, u32[]{:S(2)}) collective-permute-start(f32[4,8,128]{2,1,0:T(8,128)S(1)} %get-tuple-element.28), channel_id=1, source_target_pairs={{0,8},{8,0},{16,24},{24,16},{1,9},{9,1},{17,25},{25,17},{2,10},{10... | collective-permute-start | bytes 49160 | tf_op jit(solution)/shard_map/ppermute | solution.py:528
  23.2 4.7 %collective-permute-start.11 = (f32[4,8,128]{2,1,0:T(8,128)S(1)}, f32[4,8,128]{2,1,0:T(8,128)S(1)}, u32[]{:S(2)}, u32[]{:S(2)}) collective-permute-start(f32[4,8,128]{2,1,0:T(8,128)S(1)} %get-tuple-element.29), channel_id=1, source_target_pairs={{0,16},{8,24},{16,0},{24,8},{1,17},{9,25},{17,1},{25,9},{2,18},{10... | collective-permute-start | bytes 49160 | tf_op jit(solution)/shard_map/ppermute | solution.py:528
  25.8 5.5 %collective-permute-start.12 = (f32[4,8,128]{2,1,0:T(8,128)S(1)}, f32[4,8,128]{2,1,0:T(8,128)S(1)}, u32[]{:S(2)}, u32[]{:S(2)}) collective-permute-start(f32[4,8,128]{2,1,0:T(8,128)S(1)} %get-tuple-element.30), channel_id=1, source_target_pairs={{0,24},{8,16},{16,8},{24,0},{1,25},{9,17},{17,9},{25,1},{2,26},{10... | collective-permute-start | bytes 49160 | tf_op jit(solution)/shard_map/ppermute | solution.py:528
where the time goes:
time: 32.3 us; the launch traced here: 32.1 us
  starting transfers between devices  14.6 us (45%)
  waiting for transfers between devices  8.54 us (26%)
  Pallas kernels  7.88 us (24%)
  local copies, waits for them, and re-layouts  1.02 us (3%)
    ppermute x10, starting transfers between devices, exchange(): return lax.ppermute(x, 'space', pairs)  10.2 us
    ppermute x3, waiting for transfers between devices, iteration(): lax.ppermute(x, 'cuts', [(i, partner(i, k, slices)) for i in range(slices)])  4.83 us
    ppermute x3, starting transfers between devices, iteration(): lax.ppermute(x, 'cuts', [(i, partner(i, k, slices)) for i in range(slices)])  4.45 us
    pallas_call x1, Pallas kernels, fine_call(): pl.pallas_call(fine_kernel, out_shape=(jax.ShapeDtypeStruct((tiles, rows,...  3.8 us
    ppermute x10, waiting for transfers between devices, exchange(): return lax.ppermute(x, 'space', pairs)  3.7 us
    pallas_call x1, Pallas kernels, pair_chain_call(): pl.pallas_call(functools.partial(pair_chain_kernel, slices, rows), out_sh...  1.69 us
    pallas_call x1, Pallas kernels, pre_call(): pl.pallas_call(pre_kernel, out_shape=(jax.ShapeDtypeStruct((tiles // BLOC...  1.05 us
    slice x2, local copies, waits for them, and re-layouts, iteration(): high = exchange(jnp.concatenate([state[:REACH], stream[:REACH]]), down)  0.93 us
  transfers between devices with their start and end apart: 13, of which 6 were waited for; matrix products, arithmetic and copies ran while one was open for 0% of the time, Pallas kernels for 22%

commit v1 on v0

--- a/solution.py
+++ b/solution.py
@@ -127,39 +127,92 @@
         put(k, ((sums[0] + sums[1]) + (sums[2] + sums[3])) * (1.0 / (BLOCK * BLOCK)))
 
 
-def pre_kernel(states, stream, out, *tall):
+def rows_kernel(states, stream, to_next, to_previous, sems):
+    rows = states.shape[0]
+    copies = [
+        pltpu.make_async_copy(
+            source.at[pl.ds(first, REACH)], out.at[pl.ds(k * REACH, REACH)], sems.at[2 * j + k]
+        )
+        for j, (out, first) in enumerate(((to_next, rows - REACH), (to_previous, 0)))
+        for k, source in enumerate((states, stream))
+    ]
+    for copy in copies:
+        copy.start()
+    for copy in copies:
+        copy.wait()
+
+
+def rows_call(states, stream):
+    out = jax.ShapeDtypeStruct((2 * REACH, states.shape[1]), jnp.float32)
+    return pl.pallas_call(
+        rows_kernel,
+        out_shape=(out, out),
+        in_specs=[pl.BlockSpec(memory_space=pltpu.HBM)] * 2,
+        out_specs=(VMEM,) * 2,
+        scratch_shapes=[pltpu.SemaphoreType.DMA((4,))],
+        compiler_params=COMPACT,
+        name="rows",
+    )(*(pltpu.with_memory_space_constraint(x, pltpu.HBM) for x in (states, stream)))
+
+
+def restrict_kernel(states, stream, out, tall):
     rows, cols = states.shape
     count = rows // BLOCK
+    lane = lane_index((count, LANES))
+    per = LANES // BLOCK
     for k, source in enumerate((states, stream)):
-
-        def keep(t, value, k=k):
-            tall[k][t] = value
-
-        def take(t, i, k=k):
-            return tall[k][t, pl.ds(i, count, stride=BLOCK)]
-
-        def put(t, value, k=k):
-            out[t, k * count : (k + 1) * count] = value
-
-        spread_tiles(source, (0, rows), keep)
-        pooled(take, cols // LANES, put)
-
-
-def pre_call(states, stream):
+        for t in range(cols // LANES):
+            tall[k, t] = source[:, t * LANES : (t + 1) * LANES]
+        for c in range(cols // LANES // BLOCK):
+            whole = jnp.zeros((count, LANES), jnp.float32)
+            for q in range(BLOCK):
+                part = [tall[k, c * BLOCK + q, pl.ds(i, count, stride=BLOCK)] for i in range(BLOCK)]
+                x = (part[0] + part[1]) + (part[2] + part[3])
+                x = x + pltpu.roll(x, LANES - 1, 1)
+                x = x + pltpu.roll(x, LANES - 2, 1)
+                x = jnp.take_along_axis(x, lane * BLOCK % LANES, axis=1)
+                whole = jnp.where(lane // per == q, x, whole)
+            out[c, k * count : (k + 1) * count] = whole * (1.0 / (BLOCK * BLOCK))
+
+
+def restrict_call(states, stream):
     rows, cols = states.shape
     tiles = cols // LANES
-    tall = jax.ShapeDtypeStruct((tiles, rows, LANES), jnp.float32)
-    return pl.pallas_call(
-        pre_kernel,
-        out_shape=(jax.ShapeDtypeStruct((tiles // BLOCK, 2 * rows // BLOCK, LANES), jnp.float32), tall, tall),
+    return pl.pallas_call(
+        restrict_kernel,
+        out_shape=jax.ShapeDtypeStruct((tiles // BLOCK, 2 * rows // BLOCK, LANES), jnp.float32),
         in_specs=[VMEM] * 2,
-        out_specs=(VMEM,) * 3,
+        out_specs=VMEM,
+        scratch_shapes=[pltpu.VMEM((2, tiles, rows, LANES), jnp.float32)],
         compiler_params=COMPACT,
         name="restrict",
     )(states, stream)
 
 
-def fine_kernel(states, stream, low, high, fine, edge_low, edge_high, e_out, a, psi, z, coefs):
+def interleave_kernel(states, stream, *tall):
+    for source, out in zip((states, stream), tall, strict=True):
+
+        def keep(t, value, out=out):
+            out[t] = value
+
+        spread_tiles(source, (0, source.shape[0]), keep)
+
+
+def interleave_call(states, stream):
+    rows, cols = states.shape
+    tall = jax.ShapeDtypeStruct((cols // LANES, rows, LANES), jnp.float32)
+    return pl.pallas_call(
+        interleave_kernel,
+        out_shape=(tall, tall),
+        in_specs=[VMEM] * 2,
+        out_specs=(VMEM,) * 2,
+        compiler_params=COMPACT,
+        name="interleave",
+    )(states, stream)
+
+
+def fine_kernel(states, stream, low, high, fine, edge_twin, edge_across, e_out, a, psi, z, coefs):
+    odd = band_of_pair() == 1
     tiles, rows, _ = states.shape
     own = SUB + REACH
     top = own + rows
@@ -202,8 +255,9 @@
         step(a, z, coefs, [rows_at(n * STAGES + k) for k in range(1, STAGES + 1)], diffusion, group)
     for t in range(tiles):
         fine[t] = a[t, own:top]
-        edge_low[t] = a[t, SUB:own]
-        edge_high[t] = a[t, top : top + REACH]
+        below, above = a[t, SUB:own], a[t, top : top + REACH]
+        edge_twin[t] = jnp.where(odd, below, above)
+        edge_across[t] = jnp.where(odd, above, below)
     spread = e_out.shape[1]
 
     def take(t, i):
@@ -293,118 +347,159 @@
     )(mine, theirs)
 
 
-def partner(n, k, size):
-    return n ^ k if size & (size - 1) == 0 else (n + k) % size
-
-
-def chain(pads, outs, rows, scratch):
-    gap, old, psi, z, coefs, powers = scratch
-    tiles, size, _ = gap.shape
-    spacing, length = float(BLOCK), FINE_DT * FINE_STEPS
-    diffusion = VISCOSITY * length / (spacing * spacing)
-    whole = (SUB, size - SUB)
-    base = SUB + pads
+def partners(slices):
+    if slices == 4:
+        return [(2, 3, 1, 0), (3, 2, 0, 1), (1, 0, 3, 2)]
+    return [tuple((i + k) % slices for i in range(slices)) for k in range(1, slices)]
+
+
+def pick(n, table):
+    return sum(jnp.where(n == i, x, 0) for i, x in enumerate(table))
+
+
+def coarse_rows(reach, rows, pads):
+    reach = min(reach + -(rows + 2 * reach) % SUB // 2, pads)
+    return (SUB + pads - reach, SUB + pads + rows + reach)
+
+
+def coarse_diffusion():
+    return VISCOSITY * FINE_DT * FINE_STEPS / (BLOCK * BLOCK)
+
+
+def prepare(psi, old, z, coefs, rows, pads, slices):
+    step_size, spacing = FINE_DT * FINE_STEPS, float(BLOCK)
+    diffusion = coarse_diffusion()
+    set_coefs(psi, coefs, (SUB, SUB + rows + 2 * pads), step_size / (4.0 * spacing * spacing), diffusion, 1)
+    reach = STAGES * slices
+    step(old, z, coefs, [coarse_rows(reach - k, rows, pads) for k in range(1, STAGES + 1)], diffusion, 1)
+
+
+def clear_edges(buffers):
+    edge = jnp.zeros((SUB, LANES), jnp.float32)
+    for buffer in buffers:
+        for t in range(buffer.shape[0]):
+            buffer[t, 0:SUB] = edge
+            buffer[t, buffer.shape[1] - SUB :] = edge
+
+
+def band_of_pair():
+    return lax.rem(lax.axis_index("space"), 2)
+
+
+def pair_prepare_kernel(slices, rows, pair, near, far, old, coefs, psi, z, wide):
+    odd = band_of_pair() == 1
+    pads = 2 * rows
+    first = pl.multiple_of(rows * band_of_pair(), SUB)
+    clear_edges((old, psi, z.at[0], z.at[1]))
+    for k, out in enumerate((old, psi)):
+        part = slice(2 * k * rows, 2 * (k + 1) * rows)
+        for t in range(out.shape[0]):
+            wide[t, 0:pads] = jnp.where(odd, far[t, part], near[t, part])
+            wide[t, pads : 2 * pads] = pair[t, part]
+            wide[t, 2 * pads : 3 * pads] = jnp.where(odd, near[t, part], far[t, part])
+            out[t, SUB : SUB + rows + 2 * pads] = wide[t, pl.ds(first, rows + 2 * pads)]
+    prepare(psi, old, z, coefs, rows, pads, slices)
+
+
+def prepare_shapes(tiles, size):
+    f32 = jnp.float32
+    return (
+        (jax.ShapeDtypeStruct((tiles, size, LANES), f32), jax.ShapeDtypeStruct((4, tiles, size, LANES), f32)),
+        [pltpu.VMEM((tiles, size, LANES), f32), pltpu.VMEM((2, tiles, size, LANES), f32)],
+    )
+
+
+def pair_prepare_call(slices, pair, near, far):
+    tiles, total, _ = pair.shape
+    rows = total // 4
+    shapes, scratch = prepare_shapes(tiles, 5 * rows + 2 * SUB)
+    return pl.pallas_call(
+        functools.partial(pair_prepare_kernel, slices, rows),
+        out_shape=shapes,
+        in_specs=[VMEM] * 3,
+        out_specs=(VMEM,) * 2,
+        scratch_shapes=scratch + [pltpu.VMEM((tiles, 6 * rows, LANES), jnp.float32)],
+        compiler_params=COMPACT,
+        name="prepare",
+    )(pair, near, far)
+
+
+def chain(gap, old, z, coefs, powers, outs, rows, pads):
     slices = len(outs)
-    own = base + pl.multiple_of(rows * lax.rem(lax.axis_index("space"), 2), SUB)
-    group = 1
-    set_coefs(psi, coefs, whole, length / (2.0 * spacing) / (2.0 * spacing), diffusion, group)
-    step(old, z, coefs, [whole] * STAGES, diffusion, group)
     n = lax.axis_index("cuts")
-    for t in range(tiles):
-        start = jnp.where(n == 0, old[t, whole[0] : whole[1]], 0.0)
-        gap[t, whole[0] : whole[1]] = (gap[t, whole[0] : whole[1]] - old[t, whole[0] : whole[1]]) + start
-        mine = old[t, pl.ds(own, rows)]
+    own = slice(SUB + pads, SUB + pads + rows)
+    extent = slice(*coarse_rows(STAGES * (slices - 1), rows, pads))
+    for t in range(gap.shape[0]):
+        start = jnp.where(n == 0, old[t, extent], 0.0)
+        gap[t, extent] = (gap[t, extent] - old[t, extent]) + start
+        mine = old[t, own]
         outs[-1][t] = jnp.where(n == 0, mine, 0.0) - mine
     reach = STAGES * (slices - 1)
-
-    def around(extent):
-        extent = min(-(-extent // SUB) * SUB, pads)
-        return (base - extent, base + 2 * rows + extent)
-
     for j in range(1, slices):
+        step(gap, z, coefs, [coarse_rows(reach - k, rows, pads) for k in range(1, STAGES + 1)], coarse_diffusion(), 1)
         reach -= STAGES
-        step(gap, z, coefs, [around(reach + STAGES - k) for k in range(1, STAGES + 1)], diffusion, group)
-        for t in range(tiles):
-            powers[j, t] = gap[t, pl.ds(own, rows)]
-    for k in range(1, slices):
-        ahead = jnp.clip(partner(n, k, slices) - n, 1, slices - 1)
-        for t in range(tiles):
-            outs[k - 1][t] = powers[ahead, t]
-
-
-def pair_chain_kernel(slices, rows, whole, message, passed, coarse, coarse_near, coarse_far, *refs):
-    outs, scratch = refs[:slices], refs[slices:]
-    gap, old, psi, z = scratch[:4]
-    tiles = gap.shape[0]
-    size = gap.shape[1]
-    odd = lax.rem(lax.axis_index("space"), 2) == 1
+        for t in range(gap.shape[0]):
+            powers[j, t] = gap[t, own]
+    for out, table in zip(outs[:-1], partners(slices), strict=True):
+        ahead = pick(n, [max(x - i, 1) for i, x in enumerate(table)])
+        for t in range(gap.shape[0]):
+            out[t] = powers[ahead, t]
+
+
+def pair_chain_kernel(slices, rows, whole, message, passed, old, coefs, *refs):
+    outs, (gap, z, powers, wide) = refs[:slices], refs[slices:]
+    odd = band_of_pair() == 1
     pads = 2 * rows
-    base = SUB + pads
-    edge = jnp.zeros((SUB, LANES), jnp.float32)
-    for t in range(tiles):
-        before, after = jnp.where(odd, passed[t], message[t]), jnp.where(odd, message[t], passed[t])
-        gap[t] = jnp.zeros((size, LANES), jnp.float32)
-        at = base - SPILL
-        gap[t, at : at + whole.shape[1]] = whole[t]
-        at = base + SPILL - 2 * rows
-        gap[t, at : at + 2 * rows] = gap[t, at : at + 2 * rows] + before
-        at = base - SPILL + 2 * rows
-        gap[t, at : at + 2 * rows] = gap[t, at : at + 2 * rows] + after
-        before = jnp.where(odd, coarse_far[t], coarse_near[t])
-        after = jnp.where(odd, coarse_near[t], coarse_far[t])
-        for k, out in ((0, old), (1, psi)):
-            part = slice(2 * k * rows, 2 * (k + 1) * rows)
-            out[t, 0:SUB] = edge
-            out[t, SUB:base] = before[part]
-            out[t, base : base + 2 * rows] = coarse[t, part]
-            out[t, base + 2 * rows : base + 4 * rows] = after[part]
-            out[t, size - SUB : size] = edge
-        for k in range(2):
-            z[k, t, 0:SUB] = edge
-            z[k, t, size - SUB : size] = edge
-    chain(pads, outs, rows, scratch)
-
-
-def chain_scratch(tiles, size, slices, rows):
+    first = pl.multiple_of(rows * band_of_pair(), SUB)
+    clear_edges((gap, z.at[0], z.at[1]))
+    for t in range(gap.shape[0]):
+        wide[t] = jnp.zeros(wide.shape[1:], jnp.float32)
+        at = pads - SPILL
+        wide[t, at : at + whole.shape[1]] = whole[t]
+        for at, x in (
+            (pads + SPILL - 2 * rows, jnp.where(odd, passed[t], message[t])),
+            (pads - SPILL + 2 * rows, jnp.where(odd, message[t], passed[t])),
+        ):
+            wide[t, at : at + 2 * rows] = wide[t, at : at + 2 * rows] + x
+        gap[t, SUB : SUB + rows + 2 * pads] = wide[t, pl.ds(first, rows + 2 * pads)]
+    chain(gap, old, z, coefs, powers, outs, rows, pads)
+
+
+def chain_shapes(tiles, size, slices, rows):
     f32 = jnp.float32
-    return [
-        pltpu.VMEM((tiles, size, LANES), f32),
-        pltpu.VMEM((tiles, size, LANES), f32),
-        pltpu.VMEM((tiles, size, LANES), f32),
-        pltpu.VMEM((2, tiles, size, LANES), f32),
-        pltpu.VMEM((4, tiles, size, LANES), f32),
-        pltpu.VMEM((slices, tiles, rows, LANES), f32),
-    ]
-
-
-def pair_chain_call(slices, whole, message, passed, coarse, coarse_near, coarse_far):
+    return (
+        (jax.ShapeDtypeStruct((tiles, rows, LANES), f32),) * slices,
+        [
+            pltpu.VMEM((tiles, size, LANES), f32),
+            pltpu.VMEM((2, tiles, size, LANES), f32),
+            pltpu.VMEM((slices, tiles, rows, LANES), f32),
+        ],
+    )
+
+
+def pair_chain_call(slices, whole, message, passed, old, coefs):
     tiles = whole.shape[0]
     rows = message.shape[1] // 2
+    shapes, scratch = chain_shapes(tiles, old.shape[1], slices, rows)
     return pl.pallas_call(
         functools.partial(pair_chain_kernel, slices, rows),
-        out_shape=(jax.ShapeDtypeStruct((tiles, rows, LANES), jnp.float32),) * slices,
-        in_specs=[VMEM] * 6,
+        out_shape=shapes,
+        in_specs=[VMEM] * 5,
         out_specs=(VMEM,) * slices,
-        scratch_shapes=chain_scratch(tiles, 6 * rows + 2 * SUB, slices, rows),
+        scratch_shapes=scratch + [pltpu.VMEM((tiles, 6 * rows, LANES), jnp.float32)],
         compiler_params=COMPACT,
         name="coarse",
-    )(whole, message, passed, coarse, coarse_near, coarse_far)
-
-
-def wide_chain_kernel(slices, rows, gap_in, old_in, psi_in, *refs):
-    outs, scratch = refs[:slices], refs[slices:]
-    gap, old, psi, z = scratch[:4]
-    tiles, size, _ = gap.shape
-    edge = jnp.zeros((SUB, LANES), jnp.float32)
-    for t in range(tiles):
-        for source, out in ((gap_in, gap), (old_in, old), (psi_in, psi)):
-            out[t, 0:SUB] = edge
-            out[t, SUB : size - SUB] = source[t]
-            out[t, size - SUB : size] = edge
-        for k in range(2):
-            z[k, t, 0:SUB] = edge
-            z[k, t, size - SUB : size] = edge
-    chain((size - 2 * SUB - 2 * rows) // 2, outs, rows, scratch)
+    )(whole, message, passed, old, coefs)
+
+
+def wide_chain_kernel(slices, rows, pads, gap_in, old_in, psi_in, *refs):
+    outs, (gap, z, powers, old, coefs, psi) = refs[:slices], refs[slices:]
+    clear_edges((gap, old, psi, z.at[0], z.at[1]))
+    for source, out in ((gap_in, gap), (old_in, old), (psi_in, psi)):
+        for t in range(gap.shape[0]):
+            out[t, SUB : SUB + rows + 2 * pads] = source[t]
+    prepare(psi, old, z, coefs, rows, pads, slices)
+    chain(gap, old, z, coefs, powers, outs, rows, pads)
 
 
 def wide_chain(slices, spread, coarse):
@@ -420,33 +515,35 @@
         gap = gap.at[:, at].add(every[b])
     every = lax.all_gather(coarse, "space")
     old, psi = (jnp.moveaxis(every[:, :, k * rows : (k + 1) * rows], 0, 1).reshape(tiles, total, LANES) for k in range(2))
-    pads = STAGES * slices
-    first = lax.axis_index("space") // 2 * 2 * rows
-    at = (first - pads + jnp.arange(2 * rows + 2 * pads)) % total
-    size = 2 * rows + 2 * pads + 2 * SUB
-    return pl.pallas_call(
-        functools.partial(wide_chain_kernel, slices, rows),
-        out_shape=(jax.ShapeDtypeStruct((tiles, rows, LANES), jnp.float32),) * slices,
+    pads = -(-STAGES * slices // SUB) * SUB
+    at = (lax.axis_index("space") * rows - pads + jnp.arange(rows + 2 * pads)) % total
+    size = rows + 2 * pads + 2 * SUB
+    shapes, scratch = chain_shapes(tiles, size, slices, rows)
+    more = [pltpu.VMEM(x.shape, x.dtype) for x in prepare_shapes(tiles, size)[0]]
+    return pl.pallas_call(
+        functools.partial(wide_chain_kernel, slices, rows, pads),
+        out_shape=shapes,
         in_specs=[VMEM] * 3,
         out_specs=(VMEM,) * slices,
-        scratch_shapes=chain_scratch(tiles, size, slices, rows),
+        scratch_shapes=scratch + more + [pltpu.VMEM((tiles, size, LANES), jnp.float32)],
         compiler_params=COMPACT,
         name="coarse",
     )(*(jnp.take(x, at, axis=1) for x in (gap, old, psi)))
 
 
-def settle_kernel(fine, from_low, from_high, out, tall):
+def settle_kernel(fine, from_twin, from_across, out, tall):
     tiles, rows, _ = fine.shape
+    odd = band_of_pair() == 1
     for t in range(tiles):
-        tall[t, 0:REACH] = fine[t, 0:REACH] + from_low[t]
+        tall[t, 0:REACH] = fine[t, 0:REACH] + jnp.where(odd, from_twin[t], from_across[t])
         tall[t, REACH : rows - REACH] = fine[t, REACH : rows - REACH]
-        tall[t, rows - REACH : rows] = fine[t, rows - REACH : rows] + from_high[t]
+        tall[t, rows - REACH : rows] = fine[t, rows - REACH : rows] + jnp.where(odd, from_across[t], from_twin[t])
     for k in range(0, tiles, BLOCK):
         for i, x in enumerate(in_order([tall[k + i] for i in range(BLOCK)])):
             out[:, (k + i) * LANES : (k + i + 1) * LANES] = x
 
 
-def settle_call(fine, from_low, from_high):
+def settle_call(fine, from_twin, from_across):
     tiles, rows, _ = fine.shape
     return pl.pallas_call(
         settle_kernel,
@@ -456,7 +553,7 @@
         scratch_shapes=[pltpu.VMEM((tiles, rows, LANES), jnp.float32)],
         compiler_params=COMPACT,
         name="settle",
-    )(fine, from_low, from_high)
+    )(fine, from_twin, from_across)
 
 
 def out_kernel(slices, fine, own, *refs):
@@ -466,7 +563,7 @@
     n = lax.axis_index("cuts")
     lane = lane_index((count, LANES))
     per = LANES // BLOCK
-    sources = [(n ^ k) if slices & (slices - 1) == 0 else lax.rem(n + slices - k, slices) for k in range(1, slices)]
+    sources = [pick(n, [table.index(i) for i in range(slices)]) for table in partners(slices)]
     for k in range(cols // LANES // BLOCK):
         total = own[k]
         for source, x in zip(sources, received, strict=True):
@@ -505,28 +602,29 @@
     def exchange(x, pairs):
         return lax.ppermute(x, "space", pairs)
 
-    low = exchange(jnp.concatenate([state[-REACH:], stream[-REACH:]]), up)
-    high = exchange(jnp.concatenate([state[:REACH], stream[:REACH]]), down)
-    coarse, state, stream = pre_call(state, stream)
-    paired = bands % 2 == 0 and STAGES * (slices - 1) <= 2 * rows - SPILL
+    to_next, to_previous = rows_call(state, stream)
+    low, high = exchange(to_next, up), exchange(to_previous, down)
+    coarse = restrict_call(state, stream)
+    paired = STAGES * (slices - 1) <= 2 * rows - SPILL and STAGES * slices <= 2 * rows
     if paired:
-        coarse = pair_call(coarse, exchange(coarse, twin))
-        coarse_near = exchange(coarse, across)
-        coarse_far = exchange(coarse_near, twin)
-    fine, edge_low, edge_high, spread = fine_call(state, stream, low, high)
+        pair = pair_call(coarse, exchange(coarse, twin))
+        pair_near = exchange(pair, across)
+        pair_far = exchange(pair_near, twin)
+    tall = interleave_call(state, stream)
+    fine, edge_twin, edge_across, spread = fine_call(*tall, low, high)
     if paired:
         whole, message = spread_call(spread, exchange(spread, twin), rows)
         near = exchange(message, across)
         far = exchange(near, twin)
-        from_low, from_high = exchange(edge_high, up), exchange(edge_low, down)
-        *sent, own = pair_chain_call(slices, whole, near, far, coarse, coarse_near, coarse_far)
+        old, coefs = pair_prepare_call(slices, pair, pair_near, pair_far)
+        *sent, own = pair_chain_call(slices, whole, near, far, old, coefs)
     else:
-        from_low, from_high = exchange(edge_high, up), exchange(edge_low, down)
         *sent, own = wide_chain(slices, spread, coarse)
+    from_twin, from_across = exchange(edge_twin, twin), exchange(edge_across, across)
     received = []
-    for k, x in enumerate(sent, 1):
-        received.append(lax.ppermute(x, "cuts", [(i, partner(i, k, slices)) for i in range(slices)]))
-    return out_call(slices, settle_call(fine, from_low, from_high), own, received)
+    for x, table in zip(sent, partners(slices), strict=True):
+        received.append(lax.ppermute(x, "cuts", list(enumerate(table))))
+    return out_call(slices, settle_call(fine, from_twin, from_across), own, received)
 
 
 def solution(mesh):

time: 32.3 us -> 29.7 us (0.920)
  starting transfers between devices: 14.6 us -> 13.1 us
  waiting for transfers between devices: 8.54 us -> 7.14 us
  Pallas kernels: 7.88 us -> 9.18 us
  local copies, waits for them, and re-layouts: 1.02 us -> 0.01 us
    pallas_call x1 -> x4, Pallas kernels: 1.05 us -> 2.9 us  [the longest x1 1.03 us: rows_call(): pl.pallas_call(rows_kernel, out_shape=(out, out), in_specs=[pl.BlockSpec(...]
    ppermute x3, waiting for transfers between devices: 4.83 us -> 3.02 us  [iteration(): received.append(lax.ppermute(x, 'cuts', list(enumerate(table))))]
    ppermute x10, starting transfers between devices: 10.2 us -> 8.9 us  [exchange(): return lax.ppermute(x, 'space', pairs)]
    slice x2 -> x0, local copies, waits for them, and re-layouts: 0.93 us -> none  [iteration(): high = exchange(jnp.concatenate([state[:REACH], stream[:REACH]]), down)]
    pallas_call x1, Pallas kernels: 1.69 us -> 1.24 us  [pair_chain_call(): pl.pallas_call(functools.partial(pair_chain_kernel, slices, rows), out_sh...]
    ppermute x10, waiting for transfers between devices: 3.7 us -> 4.13 us  [exchange(): return lax.ppermute(x, 'space', pairs)]
  transfers between devices with their start and end apart: 13 -> 13, of which waited for: 6 -> 7; matrix products, arithmetic and copies ran while one was open for 0% -> 0% of each run, Pallas kernels for 22% -> 25%
where the time goes in v1:
time: 29.7 us; the launch traced here: 29.6 us
  starting transfers between devices  13.1 us (44%)
  Pallas kernels  9.18 us (31%)
  waiting for transfers between devices  7.14 us (24%)
    ppermute x10, starting transfers between devices, exchange(): return lax.ppermute(x, 'space', pairs)  8.9 us
    ppermute x3, starting transfers between devices, iteration(): received.append(lax.ppermute(x, 'cuts', list(enumerate(table))))  4.22 us
    ppermute x10, waiting for transfers between devices, exchange(): return lax.ppermute(x, 'space', pairs)  4.13 us
    pallas_call x1, Pallas kernels, fine_call(): pl.pallas_call(fine_kernel, out_shape=(jax.ShapeDtypeStruct((tiles, rows,...  3.8 us
    ppermute x3, waiting for transfers between devices, iteration(): received.append(lax.ppermute(x, 'cuts', list(enumerate(table))))  3.02 us
    pallas_call x1, Pallas kernels, pair_chain_call(): pl.pallas_call(functools.partial(pair_chain_kernel, slices, rows), out_sh...  1.24 us
    pallas_call x1, Pallas kernels, rows_call(): pl.pallas_call(rows_kernel, out_shape=(out, out), in_specs=[pl.BlockSpec(...  1.03 us
    pallas_call x1, Pallas kernels, interleave_call(): pl.pallas_call(interleave_kernel, out_shape=(tall, tall), in_specs=[VMEM]...  1 us
  transfers between devices with their start and end apart: 13, of which 7 were waited for; matrix products, arithmetic and copies ran while one was open for 0% of the time, Pallas kernels for 25%

profile of v1, /device:TPU:0, one launch (start us, length us, event | category | flops | bytes accessed | tf_op | source)
XLA Modules:
  0.0 29.6 jit_solution(8485819727735595985)
XLA Ops:
  0.0 0.0 copy-start
  0.0 0.0 copy-start.1
  0.0 1.0 %rows.1 = (f32[16,2048]{1,0:T(8,128)S(1)}, f32[16,2048]{1,0:T(8,128)S(1)}) custom-call(f32[32,2048]{1,0:T(8,128)} %bitcast.1, f32[32,2048]{1,0:T(8,128)} %stream.5), custom_call_target="tpu_custom_call" | custom-call | tf_op jit(solution)/shard_map/rows/pallas_call | solution.py:147
  1.0 0.5 %collective-permute-start = (f32[16,2048]{1,0:T(8,128)S(1)}, f32[16,2048]{1,0:T(8,128)S(1)}, u32[]{:S(2)}, u32[]{:S(2)}) collective-permute-start(f32[16,2048]{1,0:T(8,128)S(1)} %get-tuple-element.23), channel_id=1, source_target_pairs={{0,1},{1,2},{2,3},{3,4},{4,5},{5,6},{6,7},{7,0},{8,9},{9,10},{10,1... | collective-permute-start | bytes 393224 | tf_op jit(solution)/shard_map/ppermute | solution.py:603
  1.6 2.9 %collective-permute-start.1 = (f32[16,2048]{1,0:T(8,128)S(1)}, f32[16,2048]{1,0:T(8,128)S(1)}, u32[]{:S(2)}, u32[]{:S(2)}) collective-permute-start(f32[16,2048]{1,0:T(8,128)S(1)} %get-tuple-element.24), channel_id=1, source_target_pairs={{0,7},{1,0},{2,1},{3,2},{4,3},{5,4},{6,5},{7,6},{8,15},{9,8},{10,9... | collective-permute-start | bytes 393224 | tf_op jit(solution)/shard_map/ppermute | solution.py:603
  4.5 0.0 copy-done
  4.5 0.0 copy-done.1
  4.5 0.3 %restrict.1.mine = f32[4,16,128]{2,1,0:T(8,128)S(1)} custom-call(f32[32,2048]{1,0:T(8,128)S(1)} %bitcast.2, f32[32,2048]{1,0:T(8,128)S(1)} %copy-done.1), custom_call_target="tpu_custom_call" | custom-call | tf_op jit(solution)/shard_map/restrict/pallas_call | solution.py:181
  4.8 0.1 collective-permute-start.7
  4.9 1.2 %collective-permute-done.7.theirs = f32[4,16,128]{2,1,0:T(8,128)S(1)} collective-permute-done((f32[4,16,128]{2,1,0:T(8,128)S(1)}, f32[4,16,128]{2,1,0:T(8,128)S(1)}, u32[]{:S(2)}, u32[]{:S(2)}) %collective-permute-start.7) | collective-permute-done | bytes 32800 | tf_op jit(solution)/shard_map/ppermute | solution.py:603
  6.1 2.1 %collective-permute-start.8 = (f32[4,32,128]{2,1,0:T(8,128)S(1)}, f32[4,32,128]{2,1,0:T(8,128)S(1)}, u32[]{:S(2)}, u32[]{:S(2)}) collective-permute-start(f32[4,32,128]{2,1,0:T(8,128)S(1)} %pair.1), channel_id=1, source_target_pairs={{0,7},{1,2},{2,1},{3,4},{4,3},{5,6},{6,5},{7,0},{8,15},{9,10},{10,... | collective-permute-start | bytes 196616 | tf_op jit(solution)/shard_map/ppermute | solution.py:603
  8.2 1.0 %interleave.1 = (f32[16,32,128]{2,1,0:T(8,128)S(1)}, f32[16,32,128]{2,1,0:T(8,128)S(1)}) custom-call(f32[32,2048]{1,0:T(8,128)S(1)} %bitcast.3, f32[32,2048]{1,0:T(8,128)S(1)} %copy-done.1), custom_call_target="tpu_custom_call" | custom-call | tf_op jit(solution)/shard_map/interleave/pallas_call | solution.py:204
  9.2 0.0 collective-permute-done.low
  9.2 0.0 collective-permute-done.1.high
  9.2 3.8 %fine.1 = (f32[16,32,128]{2,1,0:T(8,128)S(1)}, f32[16,8,128]{2,1,0:T(8,128)S(1)}, f32[16,8,128]{2,1,0:T(8,128)S(1)}, f32[4,16,128]{2,1,0:T(8,128)S(1)}) custom-call(f32[16,32,128]{2,1,0:T(8,128)S(1)} %get-tuple-element.21.states, f32[16,32,128]{2,1,0:T(8,128)S(1)} %get-tuple-element.22.stream, f32[16,2048]{1,0:T(8,128)S(1)} %collective-permute-done.low, ...), custom_call_target="tpu_custom_call" | custom-call | tf_op jit(solution)/shard_map/fine/pallas_call | solution.py:277
  13.0 0.1 collective-permute-start.4
  13.1 0.0 collective-permute-done.8.near
  13.1 0.5 %collective-permute-start.9 = (f32[4,32,128]{2,1,0:T(8,128)S(1)}, f32[4,32,128]{2,1,0:T(8,128)S(1)}, u32[]{:S(2)}, u32[]{:S(2)}) collective-permute-start(f32[4,32,128]{2,1,0:T(8,128)S(1)} %collective-permute-done.8.near), channel_id=1, source_target_pairs={{0,1},{1,0},{2,3},{3,2},{4,5},{5,4},{6,7},{7,6},{8,9},{9,8},{10,11... | collective-permute-start | bytes 196616 | tf_op jit(solution)/shard_map/ppermute | solution.py:603
  13.6 0.7 %collective-permute-done.4.theirs = f32[4,16,128]{2,1,0:T(8,128)S(1)} collective-permute-done((f32[4,16,128]{2,1,0:T(8,128)S(1)}, f32[4,16,128]{2,1,0:T(8,128)S(1)}, u32[]{:S(2)}, u32[]{:S(2)}) %collective-permute-start.4) | collective-permute-done | bytes 32800 | tf_op jit(solution)/shard_map/ppermute | solution.py:603
  14.3 1.3 %collective-permute-start.5 = (f32[4,16,128]{2,1,0:T(8,128)S(1)}, f32[4,16,128]{2,1,0:T(8,128)S(1)}, u32[]{:S(2)}, u32[]{:S(2)}) collective-permute-start(f32[4,16,128]{2,1,0:T(8,128)S(1)} %get-tuple-element.30), channel_id=1, source_target_pairs={{0,7},{1,2},{2,1},{3,4},{4,3},{5,6},{6,5},{7,0},{8,15},{9,10},{10,... | collective-permute-start | bytes 98312 | tf_op jit(solution)/shard_map/ppermute | solution.py:603
  15.6 0.3 %collective-permute-start.2 = (f32[16,8,128]{2,1,0:T(8,128)S(1)}, f32[16,8,128]{2,1,0:T(8,128)S(1)}, u32[]{:S(2)}, u32[]{:S(2)}) collective-permute-start(f32[16,8,128]{2,1,0:T(8,128)S(1)} %get-tuple-element.26), channel_id=1, source_target_pairs={{0,1},{1,0},{2,3},{3,2},{4,5},{5,4},{6,7},{7,6},{8,9},{9,8},{10,11... | collective-permute-start | bytes 196616 | tf_op jit(solution)/shard_map/ppermute | solution.py:603
  15.9 1.1 %collective-permute-start.3 = (f32[16,8,128]{2,1,0:T(8,128)S(1)}, f32[16,8,128]{2,1,0:T(8,128)S(1)}, u32[]{:S(2)}, u32[]{:S(2)}) collective-permute-start(f32[16,8,128]{2,1,0:T(8,128)S(1)} %get-tuple-element.27), channel_id=1, source_target_pairs={{0,7},{1,2},{2,1},{3,4},{4,3},{5,6},{6,5},{7,0},{8,15},{9,10},{10,... | collective-permute-start | bytes 196616 | tf_op jit(solution)/shard_map/ppermute | solution.py:603
  17.0 1.6 %collective-permute-done.5.message = f32[4,16,128]{2,1,0:T(8,128)S(1)} collective-permute-done((f32[4,16,128]{2,1,0:T(8,128)S(1)}, f32[4,16,128]{2,1,0:T(8,128)S(1)}, u32[]{:S(2)}, u32[]{:S(2)}) %collective-permute-start.5) | collective-permute-done | bytes 32800 | tf_op jit(solution)/shard_map/ppermute | solution.py:603
  18.6 0.0 collective-permute-start.6
  18.6 0.0 collective-permute-done.9.far
  18.6 0.6 %prepare.1 = (f32[4,56,128]{2,1,0:T(8,128)S(1)}, f32[4,4,56,128]{3,2,1,0:T(8,128)S(1)}) custom-call(f32[4,32,128]{2,1,0:T(8,128)S(1)} %pair.1, f32[4,32,128]{2,1,0:T(8,128)S(1)} %collective-permute-done.8.near, f32[4,32,128]{2,1,0:T(8,128)S(1)} %collective-permute-done.9.far), custom_call_target="tpu_custom_call" | custom-call | tf_op jit(solution)/shard_map/prepare/pallas_call | solution.py:416
  19.2 0.6 %collective-permute-done.6.passed = f32[4,16,128]{2,1,0:T(8,128)S(1)} collective-permute-done((f32[4,16,128]{2,1,0:T(8,128)S(1)}, f32[4,16,128]{2,1,0:T(8,128)S(1)}, u32[]{:S(2)}, u32[]{:S(2)}) %collective-permute-start.6) | collective-permute-done | bytes 32800 | tf_op jit(solution)/shard_map/ppermute | solution.py:603
  19.8 1.2 %coarse.1 = (f32[4,8,128]{2,1,0:T(8,128)S(1)}, f32[4,8,128]{2,1,0:T(8,128)S(1)}, f32[4,8,128]{2,1,0:T(8,128)S(1)}, f32[4,8,128]{2,1,0:T(8,128)S(1)}) custom-call(f32[4,24,128]{2,1,0:T(8,128)S(1)} %get-tuple-element.29.whole, f32[4,16,128]{2,1,0:T(8,128)S(1)} %collective-permute-done.5.message, f32[4,16,128]{2,1,0:T(8,128)S(1)} %collective-permute-done.6.passed, ...), custom_call_target="tpu_custom_call" | custom-call | tf_op jit(solution)/shard_map/coarse/pallas_call | solution.py:484
  21.1 2.6 %collective-permute-start.10 = (f32[4,8,128]{2,1,0:T(8,128)S(1)}, f32[4,8,128]{2,1,0:T(8,128)S(1)}, u32[]{:S(2)}, u32[]{:S(2)}) collective-permute-start(f32[4,8,128]{2,1,0:T(8,128)S(1)} %get-tuple-element.34), channel_id=1, source_target_pairs={{0,16},{8,24},{16,8},{24,0},{1,17},{9,25},{17,9},{25,1},{2,18},{10... | collective-permute-start | bytes 49160 | tf_op jit(solution)/shard_map/ppermute | solution.py:626
  23.7 1.2 %collective-permute-start.11 = (f32[4,8,128]{2,1,0:T(8,128)S(1)}, f32[4,8,128]{2,1,0:T(8,128)S(1)}, u32[]{:S(2)}, u32[]{:S(2)}) collective-permute-start(f32[4,8,128]{2,1,0:T(8,128)S(1)} %get-tuple-element.35), channel_id=1, source_target_pairs={{0,24},{8,16},{16,0},{24,8},{1,25},{9,17},{17,1},{25,9},{2,26},{10... | collective-permute-start | bytes 49160 | tf_op jit(solution)/shard_map/ppermute | solution.py:626
  25.0 0.3 %collective-permute-start.12 = (f32[4,8,128]{2,1,0:T(8,128)S(1)}, f32[4,8,128]{2,1,0:T(8,128)S(1)}, u32[]{:S(2)}, u32[]{:S(2)}) collective-permute-start(f32[4,8,128]{2,1,0:T(8,128)S(1)} %get-tuple-element.36), channel_id=1, source_target_pairs={{0,8},{8,0},{16,24},{24,16},{1,9},{9,1},{17,25},{25,17},{2,10},{10... | collective-permute-start | bytes 49160 | tf_op jit(solution)/shard_map/ppermute | solution.py:626
  25.3 0.0 collective-permute-done.2.from_twin
  25.3 0.0 collective-permute-done.3.from_across
  25.3 0.4 %settle.1.fine = f32[32,2048]{1,0:T(8,128)S(1)} custom-call(f32[16,32,128]{2,1,0:T(8,128)S(1)} %get-tuple-element.25.fine, f32[16,8,128]{2,1,0:T(8,128)S(1)} %collective-permute-done.2.from_twin, f32[16,8,128]{2,1,0:T(8,128)S(1)} %collective-permute-done.3.from_across), custom_call_target="tpu_custom_call" | custom-call | tf_op jit(solution)/shard_map/settle/pallas_call | solution.py:548
  25.7 1.0 %collective-permute-done.10.refs_0_ = f32[4,8,128]{2,1,0:T(8,128)S(1)} collective-permute-done((f32[4,8,128]{2,1,0:T(8,128)S(1)}, f32[4,8,128]{2,1,0:T(8,128)S(1)}, u32[]{:S(2)}, u32[]{:S(2)}) %collective-permute-start.10) | collective-permute-done | bytes 16416 | tf_op jit(solution)/shard_map/ppermute | solution.py:626
  26.7 1.8 %collective-permute-done.11.refs_1_ = f32[4,8,128]{2,1,0:T(8,128)S(1)} collective-permute-done((f32[4,8,128]{2,1,0:T(8,128)S(1)}, f32[4,8,128]{2,1,0:T(8,128)S(1)}, u32[]{:S(2)}, u32[]{:S(2)}) %collective-permute-start.11) | collective-permute-done | bytes 16416 | tf_op jit(solution)/shard_map/ppermute | solution.py:626
  28.5 0.2 collective-permute-done.12.refs_2_
  28.7 0.9 %total.1 = f32[1,32,2048]{2,1,0:T(8,128)} custom-call(f32[32,2048]{1,0:T(8,128)S(1)} %settle.1.fine, f32[4,8,128]{2,1,0:T(8,128)S(1)} %get-tuple-element.33.own, f32[4,8,128]{2,1,0:T(8,128)S(1)} %collective-permute-done.10.refs_0_, f32[4,8,128]{2,1,0:T(8,128)S(1)} %collective-permute-done.11.refs_1_, f32[4,8,128]{2,1,0:T(8,128)S(1)} %collective-permute-done.12.refs_2_), custom_call_target="tpu_custom_call" | custom-call | tf_op jit(solution)/shard_map/total/pallas_call | solution.py:582
  (2 shorter events, 0.0 us)
Async XLA Ops:
  0.0 4.5 %copy-start = (f32[1,32,2048]{2,1,0:T(8,128)S(1)}, f32[1,32,2048]{2,1,0:T(8,128)}, u32[]{:S(2)}) copy-start(f32[1,32,2048]{2,1,0:T(8,128)} %param.2) | copy-start | bytes 786436
  0.0 4.5 %copy-start.1 = (f32[32,2048]{1,0:T(8,128)S(1)}, f32[32,2048]{1,0:T(8,128)}, u32[]{:S(2)}) copy-start(f32[32,2048]{1,0:T(8,128)} %stream.5) | copy-start | bytes 786436
  1.0 8.2 %collective-permute-start = (f32[16,2048]{1,0:T(8,128)S(1)}, f32[16,2048]{1,0:T(8,128)S(1)}, u32[]{:S(2)}, u32[]{:S(2)}) collective-permute-start(f32[16,2048]{1,0:T(8,128)S(1)} %get-tuple-element.23), channel_id=1, source_target_pairs={{0,1},{1,2},{2,3},{3,4},{4,5},{5,6},{6,7},{7,0},{8,9},{9,10},{10,1... | collective-permute-start | bytes 393224 | tf_op jit(solution)/shard_map/ppermute | solution.py:603
  1.6 7.6 %collective-permute-start.1 = (f32[16,2048]{1,0:T(8,128)S(1)}, f32[16,2048]{1,0:T(8,128)S(1)}, u32[]{:S(2)}, u32[]{:S(2)}) collective-permute-start(f32[16,2048]{1,0:T(8,128)S(1)} %get-tuple-element.24), channel_id=1, source_target_pairs={{0,7},{1,0},{2,1},{3,2},{4,3},{5,4},{6,5},{7,6},{8,15},{9,8},{10,9... | collective-permute-start | bytes 393224 | tf_op jit(solution)/shard_map/ppermute | solution.py:603
  4.8 1.3 %collective-permute-start.7 = (f32[4,16,128]{2,1,0:T(8,128)S(1)}, f32[4,16,128]{2,1,0:T(8,128)S(1)}, u32[]{:S(2)}, u32[]{:S(2)}) collective-permute-start(f32[4,16,128]{2,1,0:T(8,128)S(1)} %restrict.1.mine), channel_id=1, source_target_pairs={{0,1},{1,0},{2,3},{3,2},{4,5},{5,4},{6,7},{7,6},{8,9},{9,8},{10,11... | collective-permute-start | bytes 98312 | tf_op jit(solution)/shard_map/ppermute | solution.py:603
  6.1 7.0 %collective-permute-start.8 = (f32[4,32,128]{2,1,0:T(8,128)S(1)}, f32[4,32,128]{2,1,0:T(8,128)S(1)}, u32[]{:S(2)}, u32[]{:S(2)}) collective-permute-start(f32[4,32,128]{2,1,0:T(8,128)S(1)} %pair.1), channel_id=1, source_target_pairs={{0,7},{1,2},{2,1},{3,4},{4,3},{5,6},{6,5},{7,0},{8,15},{9,10},{10,... | collective-permute-start | bytes 196616 | tf_op jit(solution)/shard_map/ppermute | solution.py:603
  13.0 1.3 %collective-permute-start.4 = (f32[4,16,128]{2,1,0:T(8,128)S(1)}, f32[4,16,128]{2,1,0:T(8,128)S(1)}, u32[]{:S(2)}, u32[]{:S(2)}) collective-permute-start(f32[4,16,128]{2,1,0:T(8,128)S(1)} %get-tuple-element.28.mine), channel_id=1, source_target_pairs={{0,1},{1,0},{2,3},{3,2},{4,5},{5,4},{6,7},{7,6},{8,9},{9,8},{10,11... | collective-permute-start | bytes 98312 | tf_op jit(solution)/shard_map/ppermute | solution.py:603
  13.1 5.5 %collective-permute-start.9 = (f32[4,32,128]{2,1,0:T(8,128)S(1)}, f32[4,32,128]{2,1,0:T(8,128)S(1)}, u32[]{:S(2)}, u32[]{:S(2)}) collective-permute-start(f32[4,32,128]{2,1,0:T(8,128)S(1)} %collective-permute-done.8.near), channel_id=1, source_target_pairs={{0,1},{1,0},{2,3},{3,2},{4,5},{5,4},{6,7},{7,6},{8,9},{9,8},{10,11... | collective-permute-start | bytes 196616 | tf_op jit(solution)/shard_map/ppermute | solution.py:603
  14.3 4.3 %collective-permute-start.5 = (f32[4,16,128]{2,1,0:T(8,128)S(1)}, f32[4,16,128]{2,1,0:T(8,128)S(1)}, u32[]{:S(2)}, u32[]{:S(2)}) collective-permute-start(f32[4,16,128]{2,1,0:T(8,128)S(1)} %get-tuple-element.30), channel_id=1, source_target_pairs={{0,7},{1,2},{2,1},{3,4},{4,3},{5,6},{6,5},{7,0},{8,15},{9,10},{10,... | collective-permute-start | bytes 98312 | tf_op jit(solution)/shard_map/ppermute | solution.py:603
  15.6 9.7 %collective-permute-start.2 = (f32[16,8,128]{2,1,0:T(8,128)S(1)}, f32[16,8,128]{2,1,0:T(8,128)S(1)}, u32[]{:S(2)}, u32[]{:S(2)}) collective-permute-start(f32[16,8,128]{2,1,0:T(8,128)S(1)} %get-tuple-element.26), channel_id=1, source_target_pairs={{0,1},{1,0},{2,3},{3,2},{4,5},{5,4},{6,7},{7,6},{8,9},{9,8},{10,11... | collective-permute-start | bytes 196616 | tf_op jit(solution)/shard_map/ppermute | solution.py:603
  15.9 9.4 %collective-permute-start.3 = (f32[16,8,128]{2,1,0:T(8,128)S(1)}, f32[16,8,128]{2,1,0:T(8,128)S(1)}, u32[]{:S(2)}, u32[]{:S(2)}) collective-permute-start(f32[16,8,128]{2,1,0:T(8,128)S(1)} %get-tuple-element.27), channel_id=1, source_target_pairs={{0,7},{1,2},{2,1},{3,4},{4,3},{5,6},{6,5},{7,0},{8,15},{9,10},{10,... | collective-permute-start | bytes 196616 | tf_op jit(solution)/shard_map/ppermute | solution.py:603
  18.6 1.2 %collective-permute-start.6 = (f32[4,16,128]{2,1,0:T(8,128)S(1)}, f32[4,16,128]{2,1,0:T(8,128)S(1)}, u32[]{:S(2)}, u32[]{:S(2)}) collective-permute-start(f32[4,16,128]{2,1,0:T(8,128)S(1)} %collective-permute-done.5.message), channel_id=1, source_target_pairs={{0,1},{1,0},{2,3},{3,2},{4,5},{5,4},{6,7},{7,6},{8,9},{9,8},{10,11... | collective-permute-start | bytes 98312 | tf_op jit(solution)/shard_map/ppermute | solution.py:603
  21.1 5.6 %collective-permute-start.10 = (f32[4,8,128]{2,1,0:T(8,128)S(1)}, f32[4,8,128]{2,1,0:T(8,128)S(1)}, u32[]{:S(2)}, u32[]{:S(2)}) collective-permute-start(f32[4,8,128]{2,1,0:T(8,128)S(1)} %get-tuple-element.34), channel_id=1, source_target_pairs={{0,16},{8,24},{16,8},{24,0},{1,17},{9,25},{17,9},{25,1},{2,18},{10... | collective-permute-start | bytes 49160 | tf_op jit(solution)/shard_map/ppermute | solution.py:626
  23.7 4.7 %collective-permute-start.11 = (f32[4,8,128]{2,1,0:T(8,128)S(1)}, f32[4,8,128]{2,1,0:T(8,128)S(1)}, u32[]{:S(2)}, u32[]{:S(2)}) collective-permute-start(f32[4,8,128]{2,1,0:T(8,128)S(1)} %get-tuple-element.35), channel_id=1, source_target_pairs={{0,24},{8,16},{16,0},{24,8},{1,25},{9,17},{17,1},{25,9},{2,26},{10... | collective-permute-start | bytes 49160 | tf_op jit(solution)/shard_map/ppermute | solution.py:626
  25.0 3.7 %collective-permute-start.12 = (f32[4,8,128]{2,1,0:T(8,128)S(1)}, f32[4,8,128]{2,1,0:T(8,128)S(1)}, u32[]{:S(2)}, u32[]{:S(2)}) collective-permute-start(f32[4,8,128]{2,1,0:T(8,128)S(1)} %get-tuple-element.36), channel_id=1, source_target_pairs={{0,8},{8,0},{16,24},{24,16},{1,9},{9,1},{17,25},{25,17},{2,10},{10... | collective-permute-start | bytes 49160 | tf_op jit(solution)/shard_map/ppermute | solution.py:626

commit v2 on v1

--- a/solution.py
+++ b/solution.py
@@ -17,6 +17,7 @@
 REACH = FINE_STEPS * STAGES // 2
 SPILL = REACH // BLOCK
 VMEM = pl.BlockSpec(memory_space=pltpu.VMEM)
+CHUNK = 16
 COMPACT = pltpu.CompilerParams(vmem_limit_bytes=12 * 2**20)
 
 
@@ -72,11 +73,13 @@
 
 
 def stage(source, a, out, coefs, rows, factor, group):
-    lo, hi = rows
-    for t, east, west in neighbours(source, rows, group):
-        along = coefs[0, t, lo:hi] * east + coefs[1, t, lo:hi] * west
-        across = coefs[2, t, lo:hi] * source[t, lo + 1 : hi + 1] + coefs[3, t, lo:hi] * source[t, lo - 1 : hi - 1]
-        out[t, lo:hi] = (along + across) + factor * a[t, lo:hi]
+    chunk = CHUNK if group > 1 else rows[1] - rows[0]
+    for lo in range(*rows, chunk):
+        hi = min(lo + chunk, rows[1])
+        for t, east, west in neighbours(source, (lo, hi), group):
+            along = coefs[0, t, lo:hi] * east + coefs[1, t, lo:hi] * west
+            across = coefs[2, t, lo:hi] * source[t, lo + 1 : hi + 1] + coefs[3, t, lo:hi] * source[t, lo - 1 : hi - 1]
+            out[t, lo:hi] = (along + across) + factor * a[t, lo:hi]
 
 
 def step(a, z, coefs, rows, diffusion, group):
@@ -113,10 +116,9 @@
     return [jnp.take_along_axis(x, at, axis=1) for x in transposed(parts)]
 
 
-def spread_tiles(source, rows, put):
-    lo, hi = rows
-    for k in range(0, source.shape[1] // LANES, BLOCK):
-        parts = [source[lo:hi, (k + i) * LANES : (k + i + 1) * LANES] for i in range(BLOCK)]
+def spread_tiles(take, tiles, put):
+    for k in range(0, tiles, BLOCK):
+        parts = [take(k + i) for i in range(BLOCK)]
         for i, x in enumerate(interleaved(parts)):
             put(k + i, x)
 
@@ -127,14 +129,20 @@
         put(k, ((sums[0] + sums[1]) + (sums[2] + sums[3])) * (1.0 / (BLOCK * BLOCK)))
 
 
-def rows_kernel(states, stream, to_next, to_previous, sems):
-    rows = states.shape[0]
+def rows_kernel(states, stream, to_twin, to_across, *here):
+    here, sems = here[:2], here[2]
+    last = states.shape[0] - REACH
+    odd = band_of_pair()
     copies = [
         pltpu.make_async_copy(
-            source.at[pl.ds(first, REACH)], out.at[pl.ds(k * REACH, REACH)], sems.at[2 * j + k]
+            source.at[pl.ds(pl.multiple_of(first, SUB), REACH)], out.at[pl.ds(k * REACH, REACH)], sems.at[2 * j + k]
         )
-        for j, (out, first) in enumerate(((to_next, rows - REACH), (to_previous, 0)))
+        for j, (out, first) in enumerate(((to_twin, last * (1 - odd)), (to_across, last * odd)))
         for k, source in enumerate((states, stream))
+    ]
+    copies += [
+        pltpu.make_async_copy(source, out, sems.at[4 + k])
+        for k, (source, out) in enumerate(zip((states, stream), here, strict=True))
     ]
     for copy in copies:
         copy.start()
@@ -144,12 +152,13 @@
 
 def rows_call(states, stream):
     out = jax.ShapeDtypeStruct((2 * REACH, states.shape[1]), jnp.float32)
+    own = jax.ShapeDtypeStruct(states.shape, jnp.float32)
     return pl.pallas_call(
         rows_kernel,
-        out_shape=(out, out),
+        out_shape=(out, out, own, own),
         in_specs=[pl.BlockSpec(memory_space=pltpu.HBM)] * 2,
-        out_specs=(VMEM,) * 2,
-        scratch_shapes=[pltpu.SemaphoreType.DMA((4,))],
+        out_specs=(VMEM,) * 4,
+        scratch_shapes=[pltpu.SemaphoreType.DMA((6,))],
         compiler_params=COMPACT,
         name="rows",
     )(*(pltpu.with_memory_space_constraint(x, pltpu.HBM) for x in (states, stream)))
@@ -195,7 +204,7 @@
         def keep(t, value, out=out):
             out[t] = value
 
-        spread_tiles(source, (0, source.shape[0]), keep)
+        spread_tiles(lambda t, x=source: x[:, t * LANES : (t + 1) * LANES], source.shape[1] // LANES, keep)
 
 
 def interleave_call(states, stream):
@@ -211,13 +220,54 @@
     )(states, stream)
 
 
-def fine_kernel(states, stream, low, high, fine, edge_twin, edge_across, e_out, a, psi, z, coefs):
+def band_rows(rows):
+    own = SUB + REACH
+    spread = -(-(rows // BLOCK + 2 * SPILL) // SUB) * SUB
+    return own, own + rows, SUB + max(BLOCK * spread, rows + 2 * REACH + SUB), spread
+
+
+def inside_kernel(states, stream, levels, coefs, psi):
+    tiles, rows, _ = states.shape
+    own, top, size, _ = band_rows(rows)
+    below, above = jnp.zeros((own, LANES), jnp.float32), jnp.zeros((size - top, LANES), jnp.float32)
+    for t in range(tiles):
+        levels[0, t, own:top] = states[t]
+        psi[t, own:top] = stream[t]
+        for buffer in (psi, levels.at[0], levels.at[REACH], levels.at[REACH + 1], levels.at[REACH + 2]):
+            buffer[t, 0:own] = below
+            buffer[t, top:size] = above
+    diffusion = VISCOSITY * FINE_DT
+    set_coefs(psi, coefs, (own, top), FINE_DT * 0.25, diffusion, BLOCK)
+    _, factors = horner(diffusion)
+    for n in range(REACH):
+        base = levels.at[n // STAGES * STAGES]
+        stage(levels.at[n], base, levels.at[n + 1], coefs, (own, top), factors[n % STAGES], BLOCK)
+
+
+def inside_call(states, stream):
+    tiles, rows, _ = states.shape
+    size = band_rows(rows)[2]
+    f32 = jnp.float32
+    return pl.pallas_call(
+        inside_kernel,
+        out_shape=(
+            jax.ShapeDtypeStruct((REACH + 3, tiles, size, LANES), f32),
+            jax.ShapeDtypeStruct((4, tiles, size, LANES), f32),
+            jax.ShapeDtypeStruct((tiles, size, LANES), f32),
+        ),
+        in_specs=[VMEM] * 2,
+        out_specs=(VMEM,) * 3,
+        compiler_params=COMPACT,
+        name="inside",
+    )(states, stream)
+
+
+def fine_kernel(rows, twin, across, *refs):
+    levels, coefs, psi, fine, edge_twin, edge_across, e_out = refs[3:]
     odd = band_of_pair() == 1
-    tiles, rows, _ = states.shape
-    own = SUB + REACH
-    top = own + rows
-    size = a.shape[1]
-    for k, (buffer, source) in enumerate(((a, states), (psi, stream))):
+    tiles = psi.shape[0]
+    own, top, _, spread = band_rows(rows)
+    for k, buffer in enumerate((levels.at[0], psi)):
 
         def below(t, value, buffer=buffer):
             buffer[t, SUB:own] = value
@@ -225,40 +275,38 @@
         def above(t, value, buffer=buffer):
             buffer[t, top : top + REACH] = value
 
-        spread_tiles(low, (k * REACH, (k + 1) * REACH), below)
-        spread_tiles(high, (k * REACH, (k + 1) * REACH), above)
-        for t in range(tiles):
-            buffer[t, own:top] = source[t]
-    for t in range(tiles):
-        for buffer in (a, psi, z.at[0], z.at[1]):
-            buffer[t, 0:SUB] = jnp.zeros((SUB, LANES), jnp.float32)
-            buffer[t, top + REACH : size] = jnp.zeros((size - top - REACH, LANES), jnp.float32)
+        def received(x, y, k=k):
+            part = slice(k * REACH, (k + 1) * REACH)
+
+            def take(t):
+                at = slice(t * LANES, (t + 1) * LANES)
+                return jnp.where(odd, x[part, at], y[part, at])
+
+            return take
+
+        spread_tiles(received(twin, across), tiles, below)
+        spread_tiles(received(across, twin), tiles, above)
     diffusion = VISCOSITY * FINE_DT
-    group = BLOCK
-    set_coefs(psi, coefs, (SUB, top + REACH), FINE_DT * 0.25, diffusion, group)
+    _, factors = horner(diffusion)
+    for near in ((SUB, own + SUB), (top - SUB, top + REACH)):
+        set_coefs(psi, coefs, near, FINE_DT * 0.25, diffusion, BLOCK)
+    for n in range(REACH):
+        base = levels.at[n // STAGES * STAGES]
+        for near in ((SUB + n + 1, own + n + 1), (top - n - 1, top + REACH - n - 1)):
+            stage(levels.at[n], base, levels.at[n + 1], coefs, near, factors[n % STAGES], BLOCK)
+    a, z = levels.at[REACH], levels.at[REACH + 1 : REACH + 3]
 
     def rows_at(n):
-        reach = REACH - n if n <= REACH else n - REACH
-        spare = -(rows + 2 * reach) % SUB
-        reach += min(spare // 2, REACH - reach)
+        reach = min(n + -(rows + 2 * n) % SUB // 2, REACH)
         return (own - reach, top + reach)
 
-    half = FINE_STEPS // 2
-    for n in range(half):
-        step(a, z, coefs, [rows_at(n * STAGES + k) for k in range(1, STAGES + 1)], diffusion, group)
-    nothing = jnp.zeros((REACH, LANES), jnp.float32)
-    for t in range(tiles):
-        for buffer in (a, z.at[0], z.at[1]):
-            buffer[t, SUB:own] = nothing
-            buffer[t, top : top + REACH] = nothing
-    for n in range(half, FINE_STEPS):
-        step(a, z, coefs, [rows_at(n * STAGES + k) for k in range(1, STAGES + 1)], diffusion, group)
+    for n in range(0, REACH, STAGES):
+        step(a, z, coefs, [rows_at(n + k) for k in range(1, STAGES + 1)], diffusion, BLOCK)
     for t in range(tiles):
         fine[t] = a[t, own:top]
         below, above = a[t, SUB:own], a[t, top : top + REACH]
         edge_twin[t] = jnp.where(odd, below, above)
         edge_across[t] = jnp.where(odd, above, below)
-    spread = e_out.shape[1]
 
     def take(t, i):
         return a[t, pl.ds(SUB + i, spread, stride=BLOCK)]
@@ -269,30 +317,25 @@
     pooled(take, tiles, put)
 
 
-def fine_call(states, stream, low, high):
-    tiles, rows, _ = states.shape
-    spread = -(-(rows // BLOCK + 2 * SPILL) // SUB) * SUB
-    size = SUB + max(BLOCK * spread, rows + 2 * REACH + SUB)
+def fine_call(twin, across, levels, coefs, psi, rows):
+    tiles = psi.shape[0]
     f32 = jnp.float32
-    return pl.pallas_call(
-        fine_kernel,
-        out_shape=(
+    same = tuple(jax.ShapeDtypeStruct(x.shape, f32) for x in (levels, coefs, psi))
+    return pl.pallas_call(
+        functools.partial(fine_kernel, rows),
+        out_shape=same
+        + (
             jax.ShapeDtypeStruct((tiles, rows, LANES), f32),
             jax.ShapeDtypeStruct((tiles, REACH, LANES), f32),
             jax.ShapeDtypeStruct((tiles, REACH, LANES), f32),
-            jax.ShapeDtypeStruct((tiles // BLOCK, spread, LANES), f32),
+            jax.ShapeDtypeStruct((tiles // BLOCK, band_rows(rows)[3], LANES), f32),
         ),
-        in_specs=[VMEM] * 4,
-        out_specs=(VMEM,) * 4,
-        scratch_shapes=[
-            pltpu.VMEM((tiles, size, LANES), f32),
-            pltpu.VMEM((tiles, size, LANES), f32),
-            pltpu.VMEM((2, tiles, size, LANES), f32),
-            pltpu.VMEM((4, tiles, size, LANES), f32),
-        ],
+        in_specs=[VMEM] * 5,
+        out_specs=(VMEM,) * 7,
+        input_output_aliases={2: 0, 3: 1, 4: 2},
         compiler_params=COMPACT,
         name="fine",
-    )(states, stream, low, high)
+    )(twin, across, levels, coefs, psi)[3:]
 
 
 def pair_kernel(mine, theirs, out):
@@ -594,16 +637,14 @@
     state = states[0]
     slices, bands = lax.axis_size("cuts"), lax.axis_size("space")
     rows = state.shape[0] // BLOCK
-    up = [(i, (i + 1) % bands) for i in range(bands)]
-    down = [(i, (i - 1) % bands) for i in range(bands)]
     twin = [(i, i ^ 1) for i in range(bands)]
     across = [(i, (i + 1 if i % 2 else i - 1) % bands) for i in range(bands)]
 
     def exchange(x, pairs):
         return lax.ppermute(x, "space", pairs)
 
-    to_next, to_previous = rows_call(state, stream)
-    low, high = exchange(to_next, up), exchange(to_previous, down)
+    to_twin, to_across, state, stream = rows_call(state, stream)
+    rows_across, rows_twin = exchange(to_across, across), exchange(to_twin, twin)
     coarse = restrict_call(state, stream)
     paired = STAGES * (slices - 1) <= 2 * rows - SPILL and STAGES * slices <= 2 * rows
     if paired:
@@ -611,7 +652,8 @@
         pair_near = exchange(pair, across)
         pair_far = exchange(pair_near, twin)
     tall = interleave_call(state, stream)
-    fine, edge_twin, edge_across, spread = fine_call(*tall, low, high)
+    begun = inside_call(*tall)
+    fine, edge_twin, edge_across, spread = fine_call(rows_twin, rows_across, *begun, state.shape[0])
     if paired:
         whole, message = spread_call(spread, exchange(spread, twin), rows)
         near = exchange(message, across)

time: 29.7 us -> 28.7 us (0.966)
  starting transfers between devices: 13.1 us -> 12.1 us
    ppermute x10, starting transfers between devices: 8.9 us -> 7.91 us  [exchange(): return lax.ppermute(x, 'space', pairs)]
    pallas_call x2 -> x3, Pallas kernels: 4.83 us -> 4.83 us  [the longest x1 2.5 us: fine_call(): pl.pallas_call(functools.partial(fine_kernel, rows), out_shape=same + (ja...]
where the time goes in v2:
time: 28.7 us; the launch traced here: 28.6 us
  starting transfers between devices  12.1 us (42%)
  Pallas kernels  9.18 us (32%)
  waiting for transfers between devices  7.16 us (25%)
    ppermute x10, starting transfers between devices, exchange(): return lax.ppermute(x, 'space', pairs)  7.91 us
    ppermute x3, starting transfers between devices, iteration(): received.append(lax.ppermute(x, 'cuts', list(enumerate(table))))  4.22 us
    ppermute x10, waiting for transfers between devices, exchange(): return lax.ppermute(x, 'space', pairs)  4.14 us
    ppermute x3, waiting for transfers between devices, iteration(): received.append(lax.ppermute(x, 'cuts', list(enumerate(table))))  3.02 us
    pallas_call x1, Pallas kernels, fine_call(): pl.pallas_call(functools.partial(fine_kernel, rows), out_shape=same + (ja...  2.5 us
    pallas_call x1, Pallas kernels, pair_chain_call(): pl.pallas_call(functools.partial(pair_chain_kernel, slices, rows), out_sh...  1.24 us
    pallas_call x1, Pallas kernels, rows_call(): pl.pallas_call(rows_kernel, out_shape=(out, out, own, own), in_specs=[pl....  1.22 us
    pallas_call x1, Pallas kernels, inside_call(): pl.pallas_call(inside_kernel, out_shape=(jax.ShapeDtypeStruct((REACH + 3,...  1.11 us
  transfers between devices with their start and end apart: 13, of which 7 were waited for; matrix products, arithmetic and copies ran while one was open for 0% of the time, Pallas kernels for 25%

profile of v2, /device:TPU:0, one launch (start us, length us, event | category | flops | bytes accessed | tf_op | source)
XLA Modules:
  0.0 28.6 jit_solution(236490742729933197)
XLA Ops:
  0.0 1.2 %rows.1 = (f32[16,2048]{1,0:T(8,128)S(1)}, f32[16,2048]{1,0:T(8,128)S(1)}, f32[32,2048]{1,0:T(8,128)S(1)}, f32[32,2048]{1,0:T(8,128)S(1)}) custom-call(f32[32,2048]{1,0:T(8,128)} %bitcast.1, f32[32,2048]{1,0:T(8,128)} %stream.1), custom_call_target="tpu_custom_call" | custom-call | tf_op jit(solution)/shard_map/rows/pallas_call | solution.py:156
  1.2 0.6 %collective-permute-start = (f32[16,2048]{1,0:T(8,128)S(1)}, f32[16,2048]{1,0:T(8,128)S(1)}, u32[]{:S(2)}, u32[]{:S(2)}) collective-permute-start(f32[16,2048]{1,0:T(8,128)S(1)} %get-tuple-element.26), channel_id=1, source_target_pairs={{0,1},{1,0},{2,3},{3,2},{4,5},{5,4},{6,7},{7,6},{8,9},{9,8},{10,11... | collective-permute-start | bytes 393224 | tf_op jit(solution)/shard_map/ppermute | solution.py:644
  1.8 3.5 %collective-permute-start.1 = (f32[16,2048]{1,0:T(8,128)S(1)}, f32[16,2048]{1,0:T(8,128)S(1)}, u32[]{:S(2)}, u32[]{:S(2)}) collective-permute-start(f32[16,2048]{1,0:T(8,128)S(1)} %get-tuple-element.27), channel_id=1, source_target_pairs={{0,7},{1,2},{2,1},{3,4},{4,3},{5,6},{6,5},{7,0},{8,15},{9,10},{10,... | collective-permute-start | bytes 393224 | tf_op jit(solution)/shard_map/ppermute | solution.py:644
  5.3 0.3 %restrict.1.mine = f32[4,16,128]{2,1,0:T(8,128)S(1)} custom-call(f32[32,2048]{1,0:T(8,128)S(1)} %get-tuple-element.28.states, f32[32,2048]{1,0:T(8,128)S(1)} %get-tuple-element.29.stream), custom_call_target="tpu_custom_call" | custom-call | tf_op jit(solution)/shard_map/restrict/pallas_call | solution.py:190
  5.6 0.1 collective-permute-start.7
  5.7 1.2 %collective-permute-done.7.theirs = f32[4,16,128]{2,1,0:T(8,128)S(1)} collective-permute-done((f32[4,16,128]{2,1,0:T(8,128)S(1)}, f32[4,16,128]{2,1,0:T(8,128)S(1)}, u32[]{:S(2)}, u32[]{:S(2)}) %collective-permute-start.7) | collective-permute-done | bytes 32800 | tf_op jit(solution)/shard_map/ppermute | solution.py:644
  6.9 0.4 %collective-permute-start.8 = (f32[4,32,128]{2,1,0:T(8,128)S(1)}, f32[4,32,128]{2,1,0:T(8,128)S(1)}, u32[]{:S(2)}, u32[]{:S(2)}) collective-permute-start(f32[4,32,128]{2,1,0:T(8,128)S(1)} %pair.1), channel_id=1, source_target_pairs={{0,7},{1,2},{2,1},{3,4},{4,3},{5,6},{6,5},{7,0},{8,15},{9,10},{10,... | collective-permute-start | bytes 196616 | tf_op jit(solution)/shard_map/ppermute | solution.py:644
  7.3 1.0 %interleave.1 = (f32[16,32,128]{2,1,0:T(8,128)S(1)}, f32[16,32,128]{2,1,0:T(8,128)S(1)}) custom-call(f32[32,2048]{1,0:T(8,128)S(1)} %get-tuple-element.28.states, f32[32,2048]{1,0:T(8,128)S(1)} %get-tuple-element.29.stream), custom_call_target="tpu_custom_call" | custom-call | tf_op jit(solution)/shard_map/interleave/pallas_call | solution.py:213
  8.3 1.1 %inside.1 = (f32[11,16,72,128]{3,2,1,0:T(8,128)S(1)}, f32[4,16,72,128]{3,2,1,0:T(8,128)S(1)}, f32[16,72,128]{2,1,0:T(8,128)S(1)}) custom-call(f32[16,32,128]{2,1,0:T(8,128)S(1)} %get-tuple-element.30.states, f32[16,32,128]{2,1,0:T(8,128)S(1)} %get-tuple-element.31.stream), custom_call_target="tpu_custom_call" | custom-call | tf_op jit(solution)/shard_map/inside/pallas_call | solution.py:251
  9.4 0.0 collective-permute-done.twin
  9.4 0.0 collective-permute-done.1.across
  9.4 2.5 %fine.1 = (f32[11,16,72,128]{3,2,1,0:T(8,128)S(1)}, f32[4,16,72,128]{3,2,1,0:T(8,128)S(1)}, f32[16,72,128]{2,1,0:T(8,128)S(1)}, f32[16,32,128]{2,1,0:T(8,128)S(1...) custom-call(f32[16,2048]{1,0:T(8,128)S(1)} %collective-permute-done., ...), custom_call_target="tpu_custom_call", output_to_operand_aliasing={{0}: (2, {}), {1}: (3, {}), {2}: (4, {})} | custom-call | tf_op jit(solution)/shard_map/fine/pallas_call | solution.py:324
  12.0 0.1 collective-permute-start.4
  12.1 0.0 collective-permute-done.8.near
  12.1 0.4 %collective-permute-start.9 = (f32[4,32,128]{2,1,0:T(8,128)S(1)}, f32[4,32,128]{2,1,0:T(8,128)S(1)}, u32[]{:S(2)}, u32[]{:S(2)}) collective-permute-start(f32[4,32,128]{2,1,0:T(8,128)S(1)} %collective-permute-done.8.near), channel_id=1, source_target_pairs={{0,1},{1,0},{2,3},{3,2},{4,5},{5,4},{6,7},{7,6},{8,9},{9,8},{10,11... | collective-permute-start | bytes 196616 | tf_op jit(solution)/shard_map/ppermute | solution.py:644
  12.5 0.7 %collective-permute-done.4.theirs = f32[4,16,128]{2,1,0:T(8,128)S(1)} collective-permute-done((f32[4,16,128]{2,1,0:T(8,128)S(1)}, f32[4,16,128]{2,1,0:T(8,128)S(1)}, u32[]{:S(2)}, u32[]{:S(2)}) %collective-permute-start.4) | collective-permute-done | bytes 32800 | tf_op jit(solution)/shard_map/ppermute | solution.py:644
  13.2 2.4 %collective-permute-start.5 = (f32[4,16,128]{2,1,0:T(8,128)S(1)}, f32[4,16,128]{2,1,0:T(8,128)S(1)}, u32[]{:S(2)}, u32[]{:S(2)}) collective-permute-start(f32[4,16,128]{2,1,0:T(8,128)S(1)} %get-tuple-element.40), channel_id=1, source_target_pairs={{0,7},{1,2},{2,1},{3,4},{4,3},{5,6},{6,5},{7,0},{8,15},{9,10},{10,... | collective-permute-start | bytes 98312 | tf_op jit(solution)/shard_map/ppermute | solution.py:644
  15.7 0.0 collective-permute-start.2
  15.7 0.4 %collective-permute-start.3 = (f32[16,8,128]{2,1,0:T(8,128)S(1)}, f32[16,8,128]{2,1,0:T(8,128)S(1)}, u32[]{:S(2)}, u32[]{:S(2)}) collective-permute-start(f32[16,8,128]{2,1,0:T(8,128)S(1)} %get-tuple-element.37), channel_id=1, source_target_pairs={{0,7},{1,2},{2,1},{3,4},{4,3},{5,6},{6,5},{7,0},{8,15},{9,10},{10,... | collective-permute-start | bytes 196616 | tf_op jit(solution)/shard_map/ppermute | solution.py:644
  16.0 1.6 %collective-permute-done.5.message = f32[4,16,128]{2,1,0:T(8,128)S(1)} collective-permute-done((f32[4,16,128]{2,1,0:T(8,128)S(1)}, f32[4,16,128]{2,1,0:T(8,128)S(1)}, u32[]{:S(2)}, u32[]{:S(2)}) %collective-permute-start.5) | collective-permute-done | bytes 32800 | tf_op jit(solution)/shard_map/ppermute | solution.py:644
  17.6 0.0 collective-permute-start.6
  17.6 0.0 collective-permute-done.9.far
  17.6 0.6 %prepare.1 = (f32[4,56,128]{2,1,0:T(8,128)S(1)}, f32[4,4,56,128]{3,2,1,0:T(8,128)S(1)}) custom-call(f32[4,32,128]{2,1,0:T(8,128)S(1)} %pair.1, f32[4,32,128]{2,1,0:T(8,128)S(1)} %collective-permute-done.8.near, f32[4,32,128]{2,1,0:T(8,128)S(1)} %collective-permute-done.9.far), custom_call_target="tpu_custom_call" | custom-call | tf_op jit(solution)/shard_map/prepare/pallas_call | solution.py:459
  18.2 0.6 %collective-permute-done.6.passed = f32[4,16,128]{2,1,0:T(8,128)S(1)} collective-permute-done((f32[4,16,128]{2,1,0:T(8,128)S(1)}, f32[4,16,128]{2,1,0:T(8,128)S(1)}, u32[]{:S(2)}, u32[]{:S(2)}) %collective-permute-start.6) | collective-permute-done | bytes 32800 | tf_op jit(solution)/shard_map/ppermute | solution.py:644
  18.8 1.2 %coarse.1 = (f32[4,8,128]{2,1,0:T(8,128)S(1)}, f32[4,8,128]{2,1,0:T(8,128)S(1)}, f32[4,8,128]{2,1,0:T(8,128)S(1)}, f32[4,8,128]{2,1,0:T(8,128)S(1)}) custom-call(f32[4,24,128]{2,1,0:T(8,128)S(1)} %get-tuple-element.39.whole, f32[4,16,128]{2,1,0:T(8,128)S(1)} %collective-permute-done.5.message, f32[4,16,128]{2,1,0:T(8,128)S(1)} %collective-permute-done.6.passed, ...), custom_call_target="tpu_custom_call" | custom-call | tf_op jit(solution)/shard_map/coarse/pallas_call | solution.py:527
  20.1 2.6 %collective-permute-start.10 = (f32[4,8,128]{2,1,0:T(8,128)S(1)}, f32[4,8,128]{2,1,0:T(8,128)S(1)}, u32[]{:S(2)}, u32[]{:S(2)}) collective-permute-start(f32[4,8,128]{2,1,0:T(8,128)S(1)} %get-tuple-element.44), channel_id=1, source_target_pairs={{0,16},{8,24},{16,8},{24,0},{1,17},{9,25},{17,9},{25,1},{2,18},{10... | collective-permute-start | bytes 49160 | tf_op jit(solution)/shard_map/ppermute | solution.py:668
  22.7 1.2 %collective-permute-start.11 = (f32[4,8,128]{2,1,0:T(8,128)S(1)}, f32[4,8,128]{2,1,0:T(8,128)S(1)}, u32[]{:S(2)}, u32[]{:S(2)}) collective-permute-start(f32[4,8,128]{2,1,0:T(8,128)S(1)} %get-tuple-element.45), channel_id=1, source_target_pairs={{0,24},{8,16},{16,0},{24,8},{1,25},{9,17},{17,1},{25,9},{2,26},{10... | collective-permute-start | bytes 49160 | tf_op jit(solution)/shard_map/ppermute | solution.py:668
  24.0 0.3 %collective-permute-start.12 = (f32[4,8,128]{2,1,0:T(8,128)S(1)}, f32[4,8,128]{2,1,0:T(8,128)S(1)}, u32[]{:S(2)}, u32[]{:S(2)}) collective-permute-start(f32[4,8,128]{2,1,0:T(8,128)S(1)} %get-tuple-element.46), channel_id=1, source_target_pairs={{0,8},{8,0},{16,24},{24,16},{1,9},{9,1},{17,25},{25,17},{2,10},{10... | collective-permute-start | bytes 49160 | tf_op jit(solution)/shard_map/ppermute | solution.py:668
  24.3 0.0 collective-permute-done.2.from_twin
  24.3 0.0 collective-permute-done.3.from_across
  24.3 0.4 %settle.1.fine = f32[32,2048]{1,0:T(8,128)S(1)} custom-call(f32[16,32,128]{2,1,0:T(8,128)S(1)} %get-tuple-element.35.fine, f32[16,8,128]{2,1,0:T(8,128)S(1)} %collective-permute-done.2.from_twin, f32[16,8,128]{2,1,0:T(8,128)S(1)} %collective-permute-done.3.from_across), custom_call_target="tpu_custom_call" | custom-call | tf_op jit(solution)/shard_map/settle/pallas_call | solution.py:591
  24.7 1.0 %collective-permute-done.10.refs_0_ = f32[4,8,128]{2,1,0:T(8,128)S(1)} collective-permute-done((f32[4,8,128]{2,1,0:T(8,128)S(1)}, f32[4,8,128]{2,1,0:T(8,128)S(1)}, u32[]{:S(2)}, u32[]{:S(2)}) %collective-permute-start.10) | collective-permute-done | bytes 16416 | tf_op jit(solution)/shard_map/ppermute | solution.py:668
  25.7 1.8 %collective-permute-done.11.refs_1_ = f32[4,8,128]{2,1,0:T(8,128)S(1)} collective-permute-done((f32[4,8,128]{2,1,0:T(8,128)S(1)}, f32[4,8,128]{2,1,0:T(8,128)S(1)}, u32[]{:S(2)}, u32[]{:S(2)}) %collective-permute-start.11) | collective-permute-done | bytes 16416 | tf_op jit(solution)/shard_map/ppermute | solution.py:668
  27.5 0.2 collective-permute-done.12.refs_2_
  27.7 0.9 %total.1 = f32[1,32,2048]{2,1,0:T(8,128)} custom-call(f32[32,2048]{1,0:T(8,128)S(1)} %settle.1.fine, f32[4,8,128]{2,1,0:T(8,128)S(1)} %get-tuple-element.43.own, f32[4,8,128]{2,1,0:T(8,128)S(1)} %collective-permute-done.10.refs_0_, f32[4,8,128]{2,1,0:T(8,128)S(1)} %collective-permute-done.11.refs_1_, f32[4,8,128]{2,1,0:T(8,128)S(1)} %collective-permute-done.12.refs_2_), custom_call_target="tpu_custom_call" | custom-call | tf_op jit(solution)/shard_map/total/pallas_call | solution.py:625
  (2 shorter events, 0.0 us)
Async XLA Ops:
  1.2 8.2 %collective-permute-start = (f32[16,2048]{1,0:T(8,128)S(1)}, f32[16,2048]{1,0:T(8,128)S(1)}, u32[]{:S(2)}, u32[]{:S(2)}) collective-permute-start(f32[16,2048]{1,0:T(8,128)S(1)} %get-tuple-element.26), channel_id=1, source_target_pairs={{0,1},{1,0},{2,3},{3,2},{4,5},{5,4},{6,7},{7,6},{8,9},{9,8},{10,11... | collective-permute-start | bytes 393224 | tf_op jit(solution)/shard_map/ppermute | solution.py:644
  1.8 7.7 %collective-permute-start.1 = (f32[16,2048]{1,0:T(8,128)S(1)}, f32[16,2048]{1,0:T(8,128)S(1)}, u32[]{:S(2)}, u32[]{:S(2)}) collective-permute-start(f32[16,2048]{1,0:T(8,128)S(1)} %get-tuple-element.27), channel_id=1, source_target_pairs={{0,7},{1,2},{2,1},{3,4},{4,3},{5,6},{6,5},{7,0},{8,15},{9,10},{10,... | collective-permute-start | bytes 393224 | tf_op jit(solution)/shard_map/ppermute | solution.py:644
  5.6 1.3 %collective-permute-start.7 = (f32[4,16,128]{2,1,0:T(8,128)S(1)}, f32[4,16,128]{2,1,0:T(8,128)S(1)}, u32[]{:S(2)}, u32[]{:S(2)}) collective-permute-start(f32[4,16,128]{2,1,0:T(8,128)S(1)} %restrict.1.mine), channel_id=1, source_target_pairs={{0,1},{1,0},{2,3},{3,2},{4,5},{5,4},{6,7},{7,6},{8,9},{9,8},{10,11... | collective-permute-start | bytes 98312 | tf_op jit(solution)/shard_map/ppermute | solution.py:644
  6.9 5.2 %collective-permute-start.8 = (f32[4,32,128]{2,1,0:T(8,128)S(1)}, f32[4,32,128]{2,1,0:T(8,128)S(1)}, u32[]{:S(2)}, u32[]{:S(2)}) collective-permute-start(f32[4,32,128]{2,1,0:T(8,128)S(1)} %pair.1), channel_id=1, source_target_pairs={{0,7},{1,2},{2,1},{3,4},{4,3},{5,6},{6,5},{7,0},{8,15},{9,10},{10,... | collective-permute-start | bytes 196616 | tf_op jit(solution)/shard_map/ppermute | solution.py:644
  12.0 1.3 %collective-permute-start.4 = (f32[4,16,128]{2,1,0:T(8,128)S(1)}, f32[4,16,128]{2,1,0:T(8,128)S(1)}, u32[]{:S(2)}, u32[]{:S(2)}) collective-permute-start(f32[4,16,128]{2,1,0:T(8,128)S(1)} %get-tuple-element.38.mine), channel_id=1, source_target_pairs={{0,1},{1,0},{2,3},{3,2},{4,5},{5,4},{6,7},{7,6},{8,9},{9,8},{10,11... | collective-permute-start | bytes 98312 | tf_op jit(solution)/shard_map/ppermute | solution.py:644
  12.1 5.5 %collective-permute-start.9 = (f32[4,32,128]{2,1,0:T(8,128)S(1)}, f32[4,32,128]{2,1,0:T(8,128)S(1)}, u32[]{:S(2)}, u32[]{:S(2)}) collective-permute-start(f32[4,32,128]{2,1,0:T(8,128)S(1)} %collective-permute-done.8.near), channel_id=1, source_target_pairs={{0,1},{1,0},{2,3},{3,2},{4,5},{5,4},{6,7},{7,6},{8,9},{9,8},{10,11... | collective-permute-start | bytes 196616 | tf_op jit(solution)/shard_map/ppermute | solution.py:644
  13.2 4.4 %collective-permute-start.5 = (f32[4,16,128]{2,1,0:T(8,128)S(1)}, f32[4,16,128]{2,1,0:T(8,128)S(1)}, u32[]{:S(2)}, u32[]{:S(2)}) collective-permute-start(f32[4,16,128]{2,1,0:T(8,128)S(1)} %get-tuple-element.40), channel_id=1, source_target_pairs={{0,7},{1,2},{2,1},{3,4},{4,3},{5,6},{6,5},{7,0},{8,15},{9,10},{10,... | collective-permute-start | bytes 98312 | tf_op jit(solution)/shard_map/ppermute | solution.py:644
  15.7 8.7 %collective-permute-start.2 = (f32[16,8,128]{2,1,0:T(8,128)S(1)}, f32[16,8,128]{2,1,0:T(8,128)S(1)}, u32[]{:S(2)}, u32[]{:S(2)}) collective-permute-start(f32[16,8,128]{2,1,0:T(8,128)S(1)} %get-tuple-element.36), channel_id=1, source_target_pairs={{0,1},{1,0},{2,3},{3,2},{4,5},{5,4},{6,7},{7,6},{8,9},{9,8},{10,11... | collective-permute-start | bytes 196616 | tf_op jit(solution)/shard_map/ppermute | solution.py:644
  15.7 8.7 %collective-permute-start.3 = (f32[16,8,128]{2,1,0:T(8,128)S(1)}, f32[16,8,128]{2,1,0:T(8,128)S(1)}, u32[]{:S(2)}, u32[]{:S(2)}) collective-permute-start(f32[16,8,128]{2,1,0:T(8,128)S(1)} %get-tuple-element.37), channel_id=1, source_target_pairs={{0,7},{1,2},{2,1},{3,4},{4,3},{5,6},{6,5},{7,0},{8,15},{9,10},{10,... | collective-permute-start | bytes 196616 | tf_op jit(solution)/shard_map/ppermute | solution.py:644
  17.6 1.2 %collective-permute-start.6 = (f32[4,16,128]{2,1,0:T(8,128)S(1)}, f32[4,16,128]{2,1,0:T(8,128)S(1)}, u32[]{:S(2)}, u32[]{:S(2)}) collective-permute-start(f32[4,16,128]{2,1,0:T(8,128)S(1)} %collective-permute-done.5.message), channel_id=1, source_target_pairs={{0,1},{1,0},{2,3},{3,2},{4,5},{5,4},{6,7},{7,6},{8,9},{9,8},{10,11... | collective-permute-start | bytes 98312 | tf_op jit(solution)/shard_map/ppermute | solution.py:644
  20.1 5.6 %collective-permute-start.10 = (f32[4,8,128]{2,1,0:T(8,128)S(1)}, f32[4,8,128]{2,1,0:T(8,128)S(1)}, u32[]{:S(2)}, u32[]{:S(2)}) collective-permute-start(f32[4,8,128]{2,1,0:T(8,128)S(1)} %get-tuple-element.44), channel_id=1, source_target_pairs={{0,16},{8,24},{16,8},{24,0},{1,17},{9,25},{17,9},{25,1},{2,18},{10... | collective-permute-start | bytes 49160 | tf_op jit(solution)/shard_map/ppermute | solution.py:668
  22.7 4.7 %collective-permute-start.11 = (f32[4,8,128]{2,1,0:T(8,128)S(1)}, f32[4,8,128]{2,1,0:T(8,128)S(1)}, u32[]{:S(2)}, u32[]{:S(2)}) collective-permute-start(f32[4,8,128]{2,1,0:T(8,128)S(1)} %get-tuple-element.45), channel_id=1, source_target_pairs={{0,24},{8,16},{16,0},{24,8},{1,25},{9,17},{17,1},{25,9},{2,26},{10... | collective-permute-start | bytes 49160 | tf_op jit(solution)/shard_map/ppermute | solution.py:668
  24.0 3.7 %collective-permute-start.12 = (f32[4,8,128]{2,1,0:T(8,128)S(1)}, f32[4,8,128]{2,1,0:T(8,128)S(1)}, u32[]{:S(2)}, u32[]{:S(2)}) collective-permute-start(f32[4,8,128]{2,1,0:T(8,128)S(1)} %get-tuple-element.46), channel_id=1, source_target_pairs={{0,8},{8,0},{16,24},{24,16},{1,9},{9,1},{17,25},{25,17},{2,10},{10... | collective-permute-start | bytes 49160 | tf_op jit(solution)/shard_map/ppermute | solution.py:668

commit v3 on v2

--- a/solution.py
+++ b/solution.py
@@ -37,7 +37,7 @@
     return b, [powers[k] / b**k for k in (3, 2, 1, 0)]
 
 
-def neighbours(source, rows, group):
+def neighbours(source, rows, group, begin):
     tiles = source.shape[0]
     lo, hi = rows
     lane = lane_index((hi - lo, LANES))
@@ -47,15 +47,19 @@
     def eastern(k):
         return pltpu.roll(source[k % groups * group, lo:hi], LANES - 1, 1)
 
-    east_here, west_before = eastern(0), pltpu.roll(source[tiles - 1, lo:hi], 1, 1)
-    for k in range(groups):
+    def western(k):
+        return pltpu.roll(source[k % groups * group + group - 1, lo:hi], 1, 1)
+
+    east_here, west_before = eastern(begin), western(begin - 1)
+    for k in range(begin, begin + groups):
+        k_tile = k % groups * group
         east_after = eastern(k + 1)
-        here = [source[k * group + i, lo:hi] for i in range(group)]
+        here = [source[k_tile + i, lo:hi] for i in range(group)]
         west_here = pltpu.roll(here[-1], 1, 1)
         for i in range(group):
             east = here[i + 1] if i + 1 < group else jnp.where(last, east_after, east_here)
             west = here[i - 1] if i else jnp.where(first, west_before, west_here)
-            yield k * group + i, east, west
+            yield k_tile + i, east, west
         east_here, west_before = east_after, west_here
 
 
@@ -63,7 +67,7 @@
     lo, hi = rows
     b, _ = horner(diffusion)
     scale, diffusion = scale * b, diffusion * b
-    for t, east, west in neighbours(psi, rows, group):
+    for t, east, west in neighbours(psi, rows, group, 0):
         u = scale * (psi[t, lo + 1 : hi + 1] - psi[t, lo - 1 : hi - 1])
         v = scale * (west - east)
         coefs[0, t, lo:hi] = diffusion - u
@@ -72,11 +76,11 @@
         coefs[3, t, lo:hi] = diffusion + v
 
 
-def stage(source, a, out, coefs, rows, factor, group):
+def stage(source, a, out, coefs, rows, factor, group, begin):
     chunk = CHUNK if group > 1 else rows[1] - rows[0]
     for lo in range(*rows, chunk):
         hi = min(lo + chunk, rows[1])
-        for t, east, west in neighbours(source, (lo, hi), group):
+        for t, east, west in neighbours(source, (lo, hi), group, begin):
             along = coefs[0, t, lo:hi] * east + coefs[1, t, lo:hi] * west
             across = coefs[2, t, lo:hi] * source[t, lo + 1 : hi + 1] + coefs[3, t, lo:hi] * source[t, lo - 1 : hi - 1]
             out[t, lo:hi] = (along + across) + factor * a[t, lo:hi]
@@ -86,7 +90,7 @@
     _, factors = horner(diffusion)
     for k in range(STAGES):
         source = a if k == 0 else z.at[(k - 1) % 2]
-        stage(source, a, a if k == STAGES - 1 else z.at[k % 2], coefs, rows[k], factors[k], group)
+        stage(source, a, a if k == STAGES - 1 else z.at[k % 2], coefs, rows[k], factors[k], group, k)
 
 
 def transposed(parts):
@@ -226,7 +230,37 @@
     return own, own + rows, SUB + max(BLOCK * spread, rows + 2 * REACH + SUB), spread
 
 
-def inside_kernel(states, stream, levels, coefs, psi):
+def side(rows, low, received, levels, coefs, psi):
+    own, top, _, _ = band_rows(rows)
+    tiles = psi.shape[0]
+    first = SUB if low else top
+    for k, buffer in enumerate((levels.at[0], psi)):
+
+        def take(t, k=k):
+            return received[k * REACH : (k + 1) * REACH, t * LANES : (t + 1) * LANES]
+
+        def put(t, value, buffer=buffer):
+            buffer[t, first : first + REACH] = value
+
+        spread_tiles(take, tiles, put)
+    diffusion = VISCOSITY * FINE_DT
+    _, factors = horner(diffusion)
+    set_coefs(psi, coefs, (SUB, own + SUB) if low else (top - SUB, top + REACH), FINE_DT * 0.25, diffusion, BLOCK)
+    for n in range(REACH):
+        base = levels.at[n // STAGES * STAGES]
+        at = SUB + n + 1 if low else top - n - 1
+        stage(levels.at[n], base, levels.at[n + 1], coefs, (at, at + REACH), factors[n % STAGES], BLOCK, n)
+
+
+def either_side(low, rows, received, levels, coefs, psi):
+    for flag in (True, False):
+
+        @pl.when(low == flag)
+        def _(flag=flag):
+            side(rows, flag, received, levels, coefs, psi)
+
+
+def inside_kernel(states, stream, twin, levels, coefs, psi):
     tiles, rows, _ = states.shape
     own, top, size, _ = band_rows(rows)
     below, above = jnp.zeros((own, LANES), jnp.float32), jnp.zeros((size - top, LANES), jnp.float32)
@@ -241,10 +275,13 @@
     _, factors = horner(diffusion)
     for n in range(REACH):
         base = levels.at[n // STAGES * STAGES]
-        stage(levels.at[n], base, levels.at[n + 1], coefs, (own, top), factors[n % STAGES], BLOCK)
-
-
-def inside_call(states, stream):
+        wider = -(rows - 2 * (n + 1)) % SUB // 2
+        at = (own + n + 1 - wider, top - n - 1 + wider)
+        stage(levels.at[n], base, levels.at[n + 1], coefs, at, factors[n % STAGES], BLOCK, n)
+    either_side(band_of_pair() == 1, rows, twin, levels, coefs, psi)
+
+
+def inside_call(states, stream, twin):
     tiles, rows, _ = states.shape
     size = band_rows(rows)[2]
     f32 = jnp.float32
@@ -255,45 +292,20 @@
             jax.ShapeDtypeStruct((4, tiles, size, LANES), f32),
             jax.ShapeDtypeStruct((tiles, size, LANES), f32),
         ),
-        in_specs=[VMEM] * 2,
+        in_specs=[VMEM] * 3,
         out_specs=(VMEM,) * 3,
         compiler_params=COMPACT,
         name="inside",
-    )(states, stream)
-
-
-def fine_kernel(rows, twin, across, *refs):
+    )(states, stream, twin)
+
+
+def fine_kernel(rows, across, *refs):
     levels, coefs, psi, fine, edge_twin, edge_across, e_out = refs[3:]
     odd = band_of_pair() == 1
     tiles = psi.shape[0]
     own, top, _, spread = band_rows(rows)
-    for k, buffer in enumerate((levels.at[0], psi)):
-
-        def below(t, value, buffer=buffer):
-            buffer[t, SUB:own] = value
-
-        def above(t, value, buffer=buffer):
-            buffer[t, top : top + REACH] = value
-
-        def received(x, y, k=k):
-            part = slice(k * REACH, (k + 1) * REACH)
-
-            def take(t):
-                at = slice(t * LANES, (t + 1) * LANES)
-                return jnp.where(odd, x[part, at], y[part, at])
-
-            return take
-
-        spread_tiles(received(twin, across), tiles, below)
-        spread_tiles(received(across, twin), tiles, above)
     diffusion = VISCOSITY * FINE_DT
-    _, factors = horner(diffusion)
-    for near in ((SUB, own + SUB), (top - SUB, top + REACH)):
-        set_coefs(psi, coefs, near, FINE_DT * 0.25, diffusion, BLOCK)
-    for n in range(REACH):
-        base = levels.at[n // STAGES * STAGES]
-        for near in ((SUB + n + 1, own + n + 1), (top - n - 1, top + REACH - n - 1)):
-            stage(levels.at[n], base, levels.at[n + 1], coefs, near, factors[n % STAGES], BLOCK)
+    either_side(band_of_pair() == 0, rows, across, levels, coefs, psi)
     a, z = levels.at[REACH], levels.at[REACH + 1 : REACH + 3]
 
     def rows_at(n):
@@ -317,7 +329,7 @@
     pooled(take, tiles, put)
 
 
-def fine_call(twin, across, levels, coefs, psi, rows):
+def fine_call(across, levels, coefs, psi, rows):
     tiles = psi.shape[0]
     f32 = jnp.float32
     same = tuple(jax.ShapeDtypeStruct(x.shape, f32) for x in (levels, coefs, psi))
@@ -330,12 +342,12 @@
             jax.ShapeDtypeStruct((tiles, REACH, LANES), f32),
             jax.ShapeDtypeStruct((tiles // BLOCK, band_rows(rows)[3], LANES), f32),
         ),
-        in_specs=[VMEM] * 5,
+        in_specs=[VMEM] * 4,
         out_specs=(VMEM,) * 7,
-        input_output_aliases={2: 0, 3: 1, 4: 2},
+        input_output_aliases={1: 0, 2: 1, 3: 2},
         compiler_params=COMPACT,
         name="fine",
-    )(twin, across, levels, coefs, psi)[3:]
+    )(across, levels, coefs, psi)[3:]
 
 
 def pair_kernel(mine, theirs, out):
@@ -652,8 +664,8 @@
         pair_near = exchange(pair, across)
         pair_far = exchange(pair_near, twin)
     tall = interleave_call(state, stream)
-    begun = inside_call(*tall)
-    fine, edge_twin, edge_across, spread = fine_call(rows_twin, rows_across, *begun, state.shape[0])
+    begun = inside_call(*tall, rows_twin)
+    fine, edge_twin, edge_across, spread = fine_call(rows_across, *begun, state.shape[0])
     if paired:
         whole, message = spread_call(spread, exchange(spread, twin), rows)
         near = exchange(message, across)

time: 28.7 us -> 29.1 us (1.014)
  Pallas kernels: 9.18 us -> 9.56 us
    pallas_call x1, Pallas kernels: 1.11 us -> 2.01 us  [inside_call(): pl.pallas_call(inside_kernel, out_shape=(jax.ShapeDtypeStruct((REACH + 3,...]
    pallas_call x1, Pallas kernels: 2.5 us -> 2.11 us  [fine_call(): pl.pallas_call(functools.partial(fine_kernel, rows), out_shape=same + (ja...]
  transfers between devices with their start and end apart: 13 -> 13, of which waited for: 7 -> 7; matrix products, arithmetic and copies ran while one was open for 0% -> 0% of each run, Pallas kernels for 25% -> 26%
where the time goes in v3:
time: 29.1 us; the launch traced here: 29 us
  starting transfers between devices  12.1 us (42%)
  Pallas kernels  9.56 us (33%)
  waiting for transfers between devices  7.2 us (25%)
    ppermute x10, starting transfers between devices, exchange(): return lax.ppermute(x, 'space', pairs)  7.91 us
    ppermute x3, starting transfers between devices, iteration(): received.append(lax.ppermute(x, 'cuts', list(enumerate(table))))  4.22 us
    ppermute x10, waiting for transfers between devices, exchange(): return lax.ppermute(x, 'space', pairs)  4.18 us
    ppermute x3, waiting for transfers between devices, iteration(): received.append(lax.ppermute(x, 'cuts', list(enumerate(table))))  3.02 us
    pallas_call x1, Pallas kernels, fine_call(): pl.pallas_call(functools.partial(fine_kernel, rows), out_shape=same + (ja...  2.11 us
    pallas_call x1, Pallas kernels, inside_call(): pl.pallas_call(inside_kernel, out_shape=(jax.ShapeDtypeStruct((REACH + 3,...  2.01 us
    pallas_call x1, Pallas kernels, rows_call(): pl.pallas_call(rows_kernel, out_shape=(out, out, own, own), in_specs=[pl....  1.22 us
    pallas_call x1, Pallas kernels, pair_chain_call(): pl.pallas_call(functools.partial(pair_chain_kernel, slices, rows), out_sh...  1.15 us
  transfers between devices with their start and end apart: 13, of which 7 were waited for; matrix products, arithmetic and copies ran while one was open for 0% of the time, Pallas kernels for 26%

profile of v3, /device:TPU:0, one launch (start us, length us, event | category | flops | bytes accessed | tf_op | source)
XLA Modules:
  0.0 29.0 jit_solution(3933637126971526249)
XLA Ops:
  0.0 1.2 %rows.1 = (f32[16,2048]{1,0:T(8,128)S(1)}, f32[16,2048]{1,0:T(8,128)S(1)}, f32[32,2048]{1,0:T(8,128)S(1)}, f32[32,2048]{1,0:T(8,128)S(1)}) custom-call(f32[32,2048]{1,0:T(8,128)} %bitcast.1, f32[32,2048]{1,0:T(8,128)} %stream.1), custom_call_target="tpu_custom_call" | custom-call | tf_op jit(solution)/shard_map/rows/pallas_call | solution.py:160
  1.2 0.6 %collective-permute-start.1 = (f32[16,2048]{1,0:T(8,128)S(1)}, f32[16,2048]{1,0:T(8,128)S(1)}, u32[]{:S(2)}, u32[]{:S(2)}) collective-permute-start(f32[16,2048]{1,0:T(8,128)S(1)} %get-tuple-element.31), channel_id=1, source_target_pairs={{0,1},{1,0},{2,3},{3,2},{4,5},{5,4},{6,7},{7,6},{8,9},{9,8},{10,11... | collective-permute-start | bytes 393224 | tf_op jit(solution)/shard_map/ppermute | solution.py:656
  1.8 3.5 %collective-permute-start = (f32[16,2048]{1,0:T(8,128)S(1)}, f32[16,2048]{1,0:T(8,128)S(1)}, u32[]{:S(2)}, u32[]{:S(2)}) collective-permute-start(f32[16,2048]{1,0:T(8,128)S(1)} %get-tuple-element.26), channel_id=1, source_target_pairs={{0,7},{1,2},{2,1},{3,4},{4,3},{5,6},{6,5},{7,0},{8,15},{9,10},{10,... | collective-permute-start | bytes 393224 | tf_op jit(solution)/shard_map/ppermute | solution.py:656
  5.3 0.3 %restrict.1.mine = f32[4,16,128]{2,1,0:T(8,128)S(1)} custom-call(f32[32,2048]{1,0:T(8,128)S(1)} %get-tuple-element.27.states, f32[32,2048]{1,0:T(8,128)S(1)} %get-tuple-element.28.stream), custom_call_target="tpu_custom_call" | custom-call | tf_op jit(solution)/shard_map/restrict/pallas_call | solution.py:194
  5.6 0.1 collective-permute-start.7
  5.7 1.2 %collective-permute-done.7.theirs = f32[4,16,128]{2,1,0:T(8,128)S(1)} collective-permute-done((f32[4,16,128]{2,1,0:T(8,128)S(1)}, f32[4,16,128]{2,1,0:T(8,128)S(1)}, u32[]{:S(2)}, u32[]{:S(2)}) %collective-permute-start.7) | collective-permute-done | bytes 32800 | tf_op jit(solution)/shard_map/ppermute | solution.py:656
  6.9 0.4 %collective-permute-start.8 = (f32[4,32,128]{2,1,0:T(8,128)S(1)}, f32[4,32,128]{2,1,0:T(8,128)S(1)}, u32[]{:S(2)}, u32[]{:S(2)}) collective-permute-start(f32[4,32,128]{2,1,0:T(8,128)S(1)} %pair.1), channel_id=1, source_target_pairs={{0,7},{1,2},{2,1},{3,4},{4,3},{5,6},{6,5},{7,0},{8,15},{9,10},{10,... | collective-permute-start | bytes 196616 | tf_op jit(solution)/shard_map/ppermute | solution.py:656
  7.3 1.0 %interleave.1 = (f32[16,32,128]{2,1,0:T(8,128)S(1)}, f32[16,32,128]{2,1,0:T(8,128)S(1)}) custom-call(f32[32,2048]{1,0:T(8,128)S(1)} %get-tuple-element.27.states, f32[32,2048]{1,0:T(8,128)S(1)} %get-tuple-element.28.stream), custom_call_target="tpu_custom_call" | custom-call | tf_op jit(solution)/shard_map/interleave/pallas_call | solution.py:217
  8.3 0.0 collective-permute-done.1.twin
  8.3 2.0 %inside.1 = (f32[11,16,72,128]{3,2,1,0:T(8,128)S(1)}, f32[4,16,72,128]{3,2,1,0:T(8,128)S(1)}, f32[16,72,128]{2,1,0:T(8,128)S(1)}) custom-call(f32[16,32,128]{2,1,0:T(8,128)S(1)} %get-tuple-element.29.states, f32[16,32,128]{2,1,0:T(8,128)S(1)} %get-tuple-element.30.stream, f32[16,2048]{1,0:T(8,128)S(1)} %collective-permute-done.1.twin), custom_call_target="tpu_custom_call" | custom-call | tf_op jit(solution)/shard_map/inside/pallas_call | solution.py:288
  10.3 0.0 collective-permute-done.across
  10.4 2.1 %fine.1 = (f32[11,16,72,128]{3,2,1,0:T(8,128)S(1)}, f32[4,16,72,128]{3,2,1,0:T(8,128)S(1)}, f32[16,72,128]{2,1,0:T(8,128)S(1)}, f32[16,32,128]{2,1,0:T(8,128)S(1...) custom-call(f32[16,2048]{1,0:T(8,128)S(1)} %collective-permute-done., ...), custom_call_target="tpu_custom_call", output_to_operand_aliasing={{0}: (1, {}), {1}: (2, {}), {2}: (3, {})} | custom-call | tf_op jit(solution)/shard_map/fine/pallas_call | solution.py:336
  12.5 0.2 collective-permute-start.4
  12.6 0.0 collective-permute-done.8.near
  12.6 0.4 %collective-permute-start.9 = (f32[4,32,128]{2,1,0:T(8,128)S(1)}, f32[4,32,128]{2,1,0:T(8,128)S(1)}, u32[]{:S(2)}, u32[]{:S(2)}) collective-permute-start(f32[4,32,128]{2,1,0:T(8,128)S(1)} %collective-permute-done.8.near), channel_id=1, source_target_pairs={{0,1},{1,0},{2,3},{3,2},{4,5},{5,4},{6,7},{7,6},{8,9},{9,8},{10,11... | collective-permute-start | bytes 196616 | tf_op jit(solution)/shard_map/ppermute | solution.py:656
  13.0 0.7 %collective-permute-done.4.theirs = f32[4,16,128]{2,1,0:T(8,128)S(1)} collective-permute-done((f32[4,16,128]{2,1,0:T(8,128)S(1)}, f32[4,16,128]{2,1,0:T(8,128)S(1)}, u32[]{:S(2)}, u32[]{:S(2)}) %collective-permute-start.4) | collective-permute-done | bytes 32800 | tf_op jit(solution)/shard_map/ppermute | solution.py:656
  13.8 2.4 %collective-permute-start.5 = (f32[4,16,128]{2,1,0:T(8,128)S(1)}, f32[4,16,128]{2,1,0:T(8,128)S(1)}, u32[]{:S(2)}, u32[]{:S(2)}) collective-permute-start(f32[4,16,128]{2,1,0:T(8,128)S(1)} %get-tuple-element.40), channel_id=1, source_target_pairs={{0,7},{1,2},{2,1},{3,4},{4,3},{5,6},{6,5},{7,0},{8,15},{9,10},{10,... | collective-permute-start | bytes 98312 | tf_op jit(solution)/shard_map/ppermute | solution.py:656
  16.2 0.0 collective-permute-start.2
  16.2 0.4 %collective-permute-start.3 = (f32[16,8,128]{2,1,0:T(8,128)S(1)}, f32[16,8,128]{2,1,0:T(8,128)S(1)}, u32[]{:S(2)}, u32[]{:S(2)}) collective-permute-start(f32[16,8,128]{2,1,0:T(8,128)S(1)} %get-tuple-element.37), channel_id=1, source_target_pairs={{0,7},{1,2},{2,1},{3,4},{4,3},{5,6},{6,5},{7,0},{8,15},{9,10},{10,... | collective-permute-start | bytes 196616 | tf_op jit(solution)/shard_map/ppermute | solution.py:656
  16.5 1.6 %collective-permute-done.5.message = f32[4,16,128]{2,1,0:T(8,128)S(1)} collective-permute-done((f32[4,16,128]{2,1,0:T(8,128)S(1)}, f32[4,16,128]{2,1,0:T(8,128)S(1)}, u32[]{:S(2)}, u32[]{:S(2)}) %collective-permute-start.5) | collective-permute-done | bytes 32800 | tf_op jit(solution)/shard_map/ppermute | solution.py:656
  18.1 0.0 collective-permute-start.6
  18.1 0.0 collective-permute-done.9.far
  18.2 0.5 %prepare.1 = (f32[4,56,128]{2,1,0:T(8,128)S(1)}, f32[4,4,56,128]{3,2,1,0:T(8,128)S(1)}) custom-call(f32[4,32,128]{2,1,0:T(8,128)S(1)} %pair.1, f32[4,32,128]{2,1,0:T(8,128)S(1)} %collective-permute-done.8.near, f32[4,32,128]{2,1,0:T(8,128)S(1)} %collective-permute-done.9.far), custom_call_target="tpu_custom_call" | custom-call | tf_op jit(solution)/shard_map/prepare/pallas_call | solution.py:471
  18.7 0.7 %collective-permute-done.6.passed = f32[4,16,128]{2,1,0:T(8,128)S(1)} collective-permute-done((f32[4,16,128]{2,1,0:T(8,128)S(1)}, f32[4,16,128]{2,1,0:T(8,128)S(1)}, u32[]{:S(2)}, u32[]{:S(2)}) %collective-permute-start.6) | collective-permute-done | bytes 32800 | tf_op jit(solution)/shard_map/ppermute | solution.py:656
  19.4 1.1 %coarse.1 = (f32[4,8,128]{2,1,0:T(8,128)S(1)}, f32[4,8,128]{2,1,0:T(8,128)S(1)}, f32[4,8,128]{2,1,0:T(8,128)S(1)}, f32[4,8,128]{2,1,0:T(8,128)S(1)}) custom-call(f32[4,24,128]{2,1,0:T(8,128)S(1)} %get-tuple-element.39.whole, f32[4,16,128]{2,1,0:T(8,128)S(1)} %collective-permute-done.5.message, f32[4,16,128]{2,1,0:T(8,128)S(1)} %collective-permute-done.6.passed, ...), custom_call_target="tpu_custom_call" | custom-call | tf_op jit(solution)/shard_map/coarse/pallas_call | solution.py:539
  20.5 2.6 %collective-permute-start.10 = (f32[4,8,128]{2,1,0:T(8,128)S(1)}, f32[4,8,128]{2,1,0:T(8,128)S(1)}, u32[]{:S(2)}, u32[]{:S(2)}) collective-permute-start(f32[4,8,128]{2,1,0:T(8,128)S(1)} %get-tuple-element.44), channel_id=1, source_target_pairs={{0,16},{8,24},{16,8},{24,0},{1,17},{9,25},{17,9},{25,1},{2,18},{10... | collective-permute-start | bytes 49160 | tf_op jit(solution)/shard_map/ppermute | solution.py:680
  23.1 1.2 %collective-permute-start.11 = (f32[4,8,128]{2,1,0:T(8,128)S(1)}, f32[4,8,128]{2,1,0:T(8,128)S(1)}, u32[]{:S(2)}, u32[]{:S(2)}) collective-permute-start(f32[4,8,128]{2,1,0:T(8,128)S(1)} %get-tuple-element.45), channel_id=1, source_target_pairs={{0,24},{8,16},{16,0},{24,8},{1,25},{9,17},{17,1},{25,9},{2,26},{10... | collective-permute-start | bytes 49160 | tf_op jit(solution)/shard_map/ppermute | solution.py:680
  24.4 0.3 %collective-permute-start.12 = (f32[4,8,128]{2,1,0:T(8,128)S(1)}, f32[4,8,128]{2,1,0:T(8,128)S(1)}, u32[]{:S(2)}, u32[]{:S(2)}) collective-permute-start(f32[4,8,128]{2,1,0:T(8,128)S(1)} %get-tuple-element.46), channel_id=1, source_target_pairs={{0,8},{8,0},{16,24},{24,16},{1,9},{9,1},{17,25},{25,17},{2,10},{10... | collective-permute-start | bytes 49160 | tf_op jit(solution)/shard_map/ppermute | solution.py:680
  24.7 0.0 collective-permute-done.2.from_twin
  24.7 0.0 collective-permute-done.3.from_across
  24.7 0.4 %settle.1.fine = f32[32,2048]{1,0:T(8,128)S(1)} custom-call(f32[16,32,128]{2,1,0:T(8,128)S(1)} %get-tuple-element.35.fine, f32[16,8,128]{2,1,0:T(8,128)S(1)} %collective-permute-done.2.from_twin, f32[16,8,128]{2,1,0:T(8,128)S(1)} %collective-permute-done.3.from_across), custom_call_target="tpu_custom_call" | custom-call | tf_op jit(solution)/shard_map/settle/pallas_call | solution.py:603
  25.1 1.0 %collective-permute-done.10.refs_0_ = f32[4,8,128]{2,1,0:T(8,128)S(1)} collective-permute-done((f32[4,8,128]{2,1,0:T(8,128)S(1)}, f32[4,8,128]{2,1,0:T(8,128)S(1)}, u32[]{:S(2)}, u32[]{:S(2)}) %collective-permute-start.10) | collective-permute-done | bytes 16416 | tf_op jit(solution)/shard_map/ppermute | solution.py:680
  26.1 1.8 %collective-permute-done.11.refs_1_ = f32[4,8,128]{2,1,0:T(8,128)S(1)} collective-permute-done((f32[4,8,128]{2,1,0:T(8,128)S(1)}, f32[4,8,128]{2,1,0:T(8,128)S(1)}, u32[]{:S(2)}, u32[]{:S(2)}) %collective-permute-start.11) | collective-permute-done | bytes 16416 | tf_op jit(solution)/shard_map/ppermute | solution.py:680
  27.9 0.2 collective-permute-done.12.refs_2_
  28.1 0.9 %total.1 = f32[1,32,2048]{2,1,0:T(8,128)} custom-call(f32[32,2048]{1,0:T(8,128)S(1)} %settle.1.fine, f32[4,8,128]{2,1,0:T(8,128)S(1)} %get-tuple-element.43.own, f32[4,8,128]{2,1,0:T(8,128)S(1)} %collective-permute-done.10.refs_0_, f32[4,8,128]{2,1,0:T(8,128)S(1)} %collective-permute-done.11.refs_1_, f32[4,8,128]{2,1,0:T(8,128)S(1)} %collective-permute-done.12.refs_2_), custom_call_target="tpu_custom_call" | custom-call | tf_op jit(solution)/shard_map/total/pallas_call | solution.py:637
  (2 shorter events, 0.0 us)
Async XLA Ops:
  1.2 7.1 %collective-permute-start.1 = (f32[16,2048]{1,0:T(8,128)S(1)}, f32[16,2048]{1,0:T(8,128)S(1)}, u32[]{:S(2)}, u32[]{:S(2)}) collective-permute-start(f32[16,2048]{1,0:T(8,128)S(1)} %get-tuple-element.31), channel_id=1, source_target_pairs={{0,1},{1,0},{2,3},{3,2},{4,5},{5,4},{6,7},{7,6},{8,9},{9,8},{10,11... | collective-permute-start | bytes 393224 | tf_op jit(solution)/shard_map/ppermute | solution.py:656
  1.8 8.6 %collective-permute-start = (f32[16,2048]{1,0:T(8,128)S(1)}, f32[16,2048]{1,0:T(8,128)S(1)}, u32[]{:S(2)}, u32[]{:S(2)}) collective-permute-start(f32[16,2048]{1,0:T(8,128)S(1)} %get-tuple-element.26), channel_id=1, source_target_pairs={{0,7},{1,2},{2,1},{3,4},{4,3},{5,6},{6,5},{7,0},{8,15},{9,10},{10,... | collective-permute-start | bytes 393224 | tf_op jit(solution)/shard_map/ppermute | solution.py:656
  5.6 1.3 %collective-permute-start.7 = (f32[4,16,128]{2,1,0:T(8,128)S(1)}, f32[4,16,128]{2,1,0:T(8,128)S(1)}, u32[]{:S(2)}, u32[]{:S(2)}) collective-permute-start(f32[4,16,128]{2,1,0:T(8,128)S(1)} %restrict.1.mine), channel_id=1, source_target_pairs={{0,1},{1,0},{2,3},{3,2},{4,5},{5,4},{6,7},{7,6},{8,9},{9,8},{10,11... | collective-permute-start | bytes 98312 | tf_op jit(solution)/shard_map/ppermute | solution.py:656
  6.9 5.7 %collective-permute-start.8 = (f32[4,32,128]{2,1,0:T(8,128)S(1)}, f32[4,32,128]{2,1,0:T(8,128)S(1)}, u32[]{:S(2)}, u32[]{:S(2)}) collective-permute-start(f32[4,32,128]{2,1,0:T(8,128)S(1)} %pair.1), channel_id=1, source_target_pairs={{0,7},{1,2},{2,1},{3,4},{4,3},{5,6},{6,5},{7,0},{8,15},{9,10},{10,... | collective-permute-start | bytes 196616 | tf_op jit(solution)/shard_map/ppermute | solution.py:656
  12.5 1.3 %collective-permute-start.4 = (f32[4,16,128]{2,1,0:T(8,128)S(1)}, f32[4,16,128]{2,1,0:T(8,128)S(1)}, u32[]{:S(2)}, u32[]{:S(2)}) collective-permute-start(f32[4,16,128]{2,1,0:T(8,128)S(1)} %get-tuple-element.38.mine), channel_id=1, source_target_pairs={{0,1},{1,0},{2,3},{3,2},{4,5},{5,4},{6,7},{7,6},{8,9},{9,8},{10,11... | collective-permute-start | bytes 98312 | tf_op jit(solution)/shard_map/ppermute | solution.py:656
  12.6 5.5 %collective-permute-start.9 = (f32[4,32,128]{2,1,0:T(8,128)S(1)}, f32[4,32,128]{2,1,0:T(8,128)S(1)}, u32[]{:S(2)}, u32[]{:S(2)}) collective-permute-start(f32[4,32,128]{2,1,0:T(8,128)S(1)} %collective-permute-done.8.near), channel_id=1, source_target_pairs={{0,1},{1,0},{2,3},{3,2},{4,5},{5,4},{6,7},{7,6},{8,9},{9,8},{10,11... | collective-permute-start | bytes 196616 | tf_op jit(solution)/shard_map/ppermute | solution.py:656
  13.8 4.4 %collective-permute-start.5 = (f32[4,16,128]{2,1,0:T(8,128)S(1)}, f32[4,16,128]{2,1,0:T(8,128)S(1)}, u32[]{:S(2)}, u32[]{:S(2)}) collective-permute-start(f32[4,16,128]{2,1,0:T(8,128)S(1)} %get-tuple-element.40), channel_id=1, source_target_pairs={{0,7},{1,2},{2,1},{3,4},{4,3},{5,6},{6,5},{7,0},{8,15},{9,10},{10,... | collective-permute-start | bytes 98312 | tf_op jit(solution)/shard_map/ppermute | solution.py:656
  16.2 8.6 %collective-permute-start.2 = (f32[16,8,128]{2,1,0:T(8,128)S(1)}, f32[16,8,128]{2,1,0:T(8,128)S(1)}, u32[]{:S(2)}, u32[]{:S(2)}) collective-permute-start(f32[16,8,128]{2,1,0:T(8,128)S(1)} %get-tuple-element.36), channel_id=1, source_target_pairs={{0,1},{1,0},{2,3},{3,2},{4,5},{5,4},{6,7},{7,6},{8,9},{9,8},{10,11... | collective-permute-start | bytes 196616 | tf_op jit(solution)/shard_map/ppermute | solution.py:656
  16.2 8.6 %collective-permute-start.3 = (f32[16,8,128]{2,1,0:T(8,128)S(1)}, f32[16,8,128]{2,1,0:T(8,128)S(1)}, u32[]{:S(2)}, u32[]{:S(2)}) collective-permute-start(f32[16,8,128]{2,1,0:T(8,128)S(1)} %get-tuple-element.37), channel_id=1, source_target_pairs={{0,7},{1,2},{2,1},{3,4},{4,3},{5,6},{6,5},{7,0},{8,15},{9,10},{10,... | collective-permute-start | bytes 196616 | tf_op jit(solution)/shard_map/ppermute | solution.py:656
  18.1 1.2 %collective-permute-start.6 = (f32[4,16,128]{2,1,0:T(8,128)S(1)}, f32[4,16,128]{2,1,0:T(8,128)S(1)}, u32[]{:S(2)}, u32[]{:S(2)}) collective-permute-start(f32[4,16,128]{2,1,0:T(8,128)S(1)} %collective-permute-done.5.message), channel_id=1, source_target_pairs={{0,1},{1,0},{2,3},{3,2},{4,5},{5,4},{6,7},{7,6},{8,9},{9,8},{10,11... | collective-permute-start | bytes 98312 | tf_op jit(solution)/shard_map/ppermute | solution.py:656
  20.5 5.6 %collective-permute-start.10 = (f32[4,8,128]{2,1,0:T(8,128)S(1)}, f32[4,8,128]{2,1,0:T(8,128)S(1)}, u32[]{:S(2)}, u32[]{:S(2)}) collective-permute-start(f32[4,8,128]{2,1,0:T(8,128)S(1)} %get-tuple-element.44), channel_id=1, source_target_pairs={{0,16},{8,24},{16,8},{24,0},{1,17},{9,25},{17,9},{25,1},{2,18},{10... | collective-permute-start | bytes 49160 | tf_op jit(solution)/shard_map/ppermute | solution.py:680
  23.1 4.7 %collective-permute-start.11 = (f32[4,8,128]{2,1,0:T(8,128)S(1)}, f32[4,8,128]{2,1,0:T(8,128)S(1)}, u32[]{:S(2)}, u32[]{:S(2)}) collective-permute-start(f32[4,8,128]{2,1,0:T(8,128)S(1)} %get-tuple-element.45), channel_id=1, source_target_pairs={{0,24},{8,16},{16,0},{24,8},{1,25},{9,17},{17,1},{25,9},{2,26},{10... | collective-permute-start | bytes 49160 | tf_op jit(solution)/shard_map/ppermute | solution.py:680
  24.4 3.7 %collective-permute-start.12 = (f32[4,8,128]{2,1,0:T(8,128)S(1)}, f32[4,8,128]{2,1,0:T(8,128)S(1)}, u32[]{:S(2)}, u32[]{:S(2)}) collective-permute-start(f32[4,8,128]{2,1,0:T(8,128)S(1)} %get-tuple-element.46), channel_id=1, source_target_pairs={{0,8},{8,0},{16,24},{24,16},{1,9},{9,1},{17,25},{25,17},{2,10},{10... | collective-permute-start | bytes 49160 | tf_op jit(solution)/shard_map/ppermute | solution.py:680
